TPU v7x, 256 devices: a whole 4x4x8 slice. The times are simulated.
256 devices in a mesh: hist: 64 (over z, y, core), rep: 4 (over x).
Axes of the slice: x: 4, y: 4, z: 8, core: 2. Of those that a mesh axis runs over, the one named last changes fastest.
Arguments:
- features: bfloat16 [4, 16384, 512], P('rep', 'hist'), may hold values from -16 to 16
- history: bfloat16 [4, 131072, 512], P('rep', 'hist'), may hold values from -6 to 6
- blk_owner: int32 [4, 1024, 1], P('rep', 'hist'), may hold values from 0 to 63; in each aligned block of 16 rows (0 to 15, 16 to 31, ..., all dimensions but the last counted through in order) at most 2 rows name the same one
- blk_offset: int32 [4, 1024], P('rep', 'hist'), may hold values from 0 to 15
- blk_relation: int32 [4, 1024], P('rep', 'hist'), may hold values from 0 to 7
- adjacency: bfloat16 [4, 1024, 128, 128], P('rep', 'hist'), may hold values from -0.5 to 0.5
- weights: bfloat16 [9, 512, 512], replicated, may hold values from -0.09375 to 0.09375
- cotangent: bfloat16 [4, 16384, 512], P('rep', 'hist'), may hold values from -6 to 6
Outputs:
- fresh: bfloat16 [4, 16384, 512], P('rep', 'hist')
- grad_features: bfloat16 [4, 16384, 512], P('rep', 'hist')
- grad_weights: float32 [9, 262144], P(None, 'hist')
Inputs may be any that keep to these rules, and one draw needn't show every extreme that they name: `blk_owner`: within the 16 rows of one device at most 2 blocks name one owner, and in every draw some owner is named by exactly 2 rows of some device.
All inputs are finite; a program needn't handle non-finite values.
Results may differ from a plain program's by a relative error of at most 0.0053.
Values may be sent and summed in bfloat16 or wider, within the bound.
A program may use at most 128 MiB of HBM per device.

v0:
```python
import jax
import jax.numpy as jnp
from jax import lax
from jax.sharding import PartitionSpec as P


def on_device(
    features, history, blk_owner, blk_offset, blk_relation, adjacency, weights, cotangent
):
    n_hist = lax.axis_size("hist")
    owners = blk_owner.reshape(-1)
    offsets = blk_offset.reshape(-1)
    relation = blk_relation.reshape(-1)
    tiles = adjacency[0]
    nblocks = owners.shape[0]
    tile_rows = tiles.shape[-1]
    width = weights.shape[-1]
    relations = weights.shape[0] - 1
    batch_tiles = features.shape[1] // tile_rows
    per_tile = nblocks // batch_tiles
    capacity = max(2, (nblocks + n_hist - 1) // n_hist)
    matches = (owners[:, None] == jnp.arange(n_hist, dtype=jnp.int32)[None, :]).astype(jnp.int32)
    position = jnp.sum((jnp.cumsum(matches, axis=0) - matches) * matches, axis=1)
    slot_index = owners * capacity + position
    request = jnp.zeros((n_hist * capacity,), jnp.int32).at[slot_index].set(offsets)
    request = request.reshape(n_hist, capacity)
    table = history.reshape(-1, tile_rows, width)
    asked = lax.all_to_all(request, "hist", split_axis=0, concat_axis=0, tiled=True)
    arrived = lax.all_to_all(table[asked], "hist", split_axis=0, concat_axis=0, tiled=True)
    pulled = arrived.reshape(n_hist * capacity, tile_rows, width)[slot_index]
    block_sum = jnp.einsum("bij,bjd->bid", tiles, pulled, preferred_element_type=jnp.float32)
    block_sum = block_sum.reshape(batch_tiles, per_tile, tile_rows, width)
    onehot = (
        relation.reshape(batch_tiles, per_tile)[:, :, None]
        == jnp.arange(relations, dtype=jnp.int32)[None, None, :]
    ).astype(jnp.float32)
    mixed = jnp.einsum("tkr,tkid->trid", onehot, block_sum, precision=lax.Precision.HIGHEST).astype(
        jnp.bfloat16
    )
    local_x = features.reshape(batch_tiles, tile_rows, width)
    local_g = cotangent.reshape(batch_tiles, tile_rows, width)
    stacked = jnp.concatenate([local_x[:, None], mixed], axis=1)
    pre = jnp.einsum("trid,rde->tie", stacked, weights, preferred_element_type=jnp.float32)
    sigma = jax.nn.sigmoid(pre)
    fresh = (local_x.astype(jnp.float32) + pre * sigma).astype(jnp.bfloat16)
    dpre = (local_g.astype(jnp.float32) * sigma * (1.0 + pre * (1.0 - sigma))).astype(jnp.bfloat16)
    grad_x = local_g.astype(jnp.float32) + jnp.einsum(
        "tie,de->tid", dpre, weights[0], preferred_element_type=jnp.float32
    )
    grad_x = grad_x.astype(jnp.bfloat16)
    grad_w = jnp.einsum("trid,tie->rde", stacked, dpre, preferred_element_type=jnp.float32)
    flat_grad = grad_w.reshape(relations + 1, width * width)
    share = lax.psum_scatter(flat_grad, "hist", scatter_dimension=1, tiled=True)
    summed = lax.psum(share, "rep")
    fresh = fresh.reshape(1, batch_tiles * tile_rows, width)
    grad_x = grad_x.reshape(1, batch_tiles * tile_rows, width)
    return (fresh, grad_x, summed)


def solution(mesh):
    in_specs = (
        P("rep", "hist", None),
        P("rep", "hist", None),
        P("rep", "hist", None),
        P("rep", "hist"),
        P("rep", "hist"),
        P("rep", "hist", None, None),
        P(),
        P("rep", "hist", None),
    )
    out_specs = (P("rep", "hist", None), P("rep", "hist", None), P(None, "hist"))
    return jax.shard_map(
        on_device, mesh=mesh, in_specs=in_specs, out_specs=out_specs, check_vma=False
    )
```

profile of v0, /device:TPU:8, one launch (start us, length us, event | category | flops | bytes accessed | tf_op | source)
XLA Modules:
  0.0 727.4 jit_solution(9442419736519274689)
XLA Ops:
  7.2 0.9 fusion.18
  8.1 0.8 select_reduce_fusion
  8.9 0.7 fusion.22
  9.6 0.8 scatter_custom_fusion
  10.5 20.5 %all_to_all.17 = s32[64,1,2]{2,1,0:T(1,128)S(1)} all-to-all(s32[64,1,2]{2,1,0:T(1,128)S(1)} %bitcast.70), channel_id=1, replica_groups=mesh['hist'=64,'rep'=4] {'hist'}, dimensions={0} | all-to-all | bytes 1024 | tf_op jit(solution)/shard_map/all_to_all | solution.py:28
  31.3 7.8 %gather_fusion = bf16[128,128,512]{2,1,0:T(8,128)(2,1)} fusion(bf16[16,128,512]{2,1,0:T(8,128)(2,1)S(1)} %bitcast.61, s32[1024]{0:T(1024)S(1)} %pad_clamp_fusion.1), kind=kCustom, calls=%fused_computation | custom fusion | bytes 33554944 | tf_op jit(solution)/shard_map/gather | solution.py:29
  39.1 6.8 all-to-all-start.1
  46.0 0.5 broadcast.78
  46.5 0.7 reduce.3
  47.3 0.4 copy.28
  47.7 368.5 %all-to-all-done.1 = bf16[64,2,128,512]{3,2,1,0:T(8,128)(2,1)} async-done(((bf16[64,2,128,512]{3,2,1,0:T(8,128)(2,1)}), bf16[64,2,128,512]{3,2,1,0:T(8,128)(2,1)}, u32[]{:S(2)}, u32[]{:S(2)}) %all-to-all-start.1) | async-done | bytes 16777248 | tf_op jit(solution)/shard_map/all_to_all | solution.py:29
  416.2 6.4 gather_fusion.1
  422.6 2.7 fusion.14
  425.3 5.5 copy.27
  430.8 4.3 convolution_convert_fusion
  435.2 2.0 pad_maximum_fusion
  437.2 6.1 fusion.12
  443.3 9.4 %convolution_bitcast_fusion = f32[9,512,512]{2,1,0:T(8,128)} fusion(bf16[2,9,128,512]{3,1,2,0:T(8,128)(2,1)S(1)} %pad_maximum_fusion, bf16[2,128,512]{2,1,0:T(8,128)(2,1)S(1)} %bitcast.68, f32[2,128,512]{2,1,0:T(8,128)S(1)} %get-tuple-element.4), kind=kOutput, calls=%fused_computation.6 | convolution fusion | flops 1209270272 | bytes 12582912 | tf_op jit(solution)/shard_map/trid,tie->rde/dot_general | solution.py:51
  452.7 11.5 %pad.4 = f32[16,512,512]{2,1,0:T(8,128)} pad(f32[9,512,512]{2,1,0:T(8,128)} %convolution_bitcast_fusion, f32[]{:T(128)} %constant.34), padding=0_7x0_0x0_0 | pad | bytes 26214404
  464.3 17.7 %copy.35 = f32[2,8,512,512]{3,1,2,0:T(8,128)} copy(f32[2,8,512,512]{3,2,1,0:T(8,128)} %bitcast.64) | data formatting | bytes 33554432
  482.1 188.4 %reduce-scatter.2.cloned.1.call-done = f32[9,4096]{1,0:T(8,128)} async-done(((f32[9,262144]{1,0:T(8,128)}), f32[9,4096]{1,0:T(8,128)}) %reduce-scatter.2.cloned.1.call-update) | async-done | bytes 147472 | tf_op jit(solution)/shard_map/reduce_scatter | solution.py:53
  670.5 2.1 fusion.9
  672.6 46.3 %all-reduce.2.cloned.1.call-done = f32[9,4096]{1,0:T(8,128)} async-done(((f32[9,4096]{1,0:T(8,128)}), f32[9,4096]{1,0:T(8,128)}) %all-reduce.2.cloned.1.call-update) | async-done | bytes 147472 | tf_op jit(solution)/shard_map/psum | solution.py:54
  718.9 1.7 copy.45
  (25 shorter events, 0.7 us)
Async XLA Ops:
  7.2 24.2 %copy-start = (bf16[1,2048,512]{2,1,0:T(8,128)(2,1)S(1)}, bf16[1,2048,512]{2,1,0:T(8,128)(2,1)}, u32[]{:S(2)}) copy-start(bf16[1,2048,512]{2,1,0:T(8,128)(2,1)} %param.9) | copy-start | bytes 6291460
  39.1 7.4 %copy-start.5 = (s32[1,16]{1,0:T(1,128)S(1)}, s32[1,16]{1,0:T(1,128)}, u32[]{:S(2)}) copy-start(s32[1,16]{1,0:T(1,128)} %param.12) | copy-start | bytes 196
  39.1 8.1 %copy-start.3 = (bf16[1,256,512]{2,1,0:T(8,128)(2,1)S(1)}, bf16[1,256,512]{2,1,0:T(8,128)(2,1)}, u32[]{:S(2)}) copy-start(bf16[1,256,512]{2,1,0:T(8,128)(2,1)} %param.8) | copy-start | bytes 786436
  39.1 377.1 %all-to-all-start.1 = ((bf16[64,2,128,512]{3,2,1,0:T(8,128)(2,1)}), bf16[64,2,128,512]{3,2,1,0:T(8,128)(2,1)}, u32[]{:S(2)}, u32[]{:S(2)}) async-start(bf16[64,2,128,512]{3,2,1,0:T(8,128)(2,1)} %bitcast.62), calls=%async_computation.1 | async-start | bytes 33554432 | tf_op jit(solution)/shard_map/all_to_all | solution.py:29
  45.9 376.7 %copy-start.2 = (bf16[1,16,128,128]{3,2,1,0:T(8,128)(2,1)S(1)}, bf16[1,16,128,128]{3,2,1,0:T(8,128)(2,1)}, u32[]{:S(2)}) copy-start(bf16[1,16,128,128]{3,2,1,0:T(8,128)(2,1)} %param.13) | copy-start | bytes 1572868
  45.9 624.5 %reduce-scatter.2.cloned.1.call-start = ((), (), s32[]{:S(2)}) async-start(), calls=%async_computation.3 | async-start | bytes 17039360 | tf_op jit(solution)/shard_map/reduce_scatter | solution.py:53
  437.2 6.1 copy-start.4
  482.0 238.6 %copy-start.1 = (bf16[1,2048,512]{2,1,0:T(8,128)(2,1)S(1)}, bf16[1,2048,512]{2,1,0:T(8,128)(2,1)}, u32[]{:S(2)}) copy-start(bf16[1,2048,512]{2,1,0:T(8,128)(2,1)} %param.9) | copy-start | bytes 6291460
  482.0 236.9 %all-reduce.2.cloned.1.call-start = ((), (), s32[]{:S(2)}) async-start(), calls=%async_computation.4 | async-start | bytes 524288 | tf_op jit(solution)/shard_map/psum | solution.py:54
Sparse Core Ops, SparseCore 0:
  482.1 188.2 reduce-scatter.1
  672.8 46.0 all-reduce.1
where the time goes:
time: 728 us; the launch traced here: 727 us
  waiting for transfers between devices  603 us (83%)
  local copies, waits for them, and re-layouts  52.9 us (7%)
  matrix products  24.7 us (3%)
  blocking collectives  20.5 us (3%)
  between operations  14.2 us (2%)
    all_to_all x1, waiting for transfers between devices, on_device(): lax.all_to_all(table[asked], 'hist', split_axis=0, concat_axis=0, tiled=T...  368 us
    reduce_scatter x1, waiting for transfers between devices, on_device(): share = lax.psum_scatter(flat_grad, 'hist', scatter_dimension=1, tiled=True)  188 us
    psum x1, waiting for transfers between devices, on_device(): summed = lax.psum(share, 'rep')  46.3 us
    unnamed x16, local copies, waits for them, and re-layouts  31.5 us
    all_to_all x1, blocking collectives, on_device(): lax.all_to_all(request, 'hist', split_axis=0, concat_axis=0, tiled=True)  20.5 us
  transfers between devices with their start and end apart: 3, of which 3 were waited for; matrix products, arithmetic and copies ran while one was open for 1% of the time, Pallas kernels for 0%

commit v1 on v0

v1 whole, which is shorter than its diff:
```python
import functools

import jax
import jax.numpy as jnp
from jax import lax
from jax.experimental import pallas as pl
from jax.experimental.pallas import tpu as pltpu
from jax.sharding import PartitionSpec as P

Y = 4
CORES = 2
PLANE = Y * CORES
CHUNKS = 4


def place(plane_count):
    me = lax.axis_index("hist")
    z, y, c = me // PLANE, (me // CORES) % Y, me % CORES

    def hist(dz=0, dy=0, dc=0):
        zz = lax.rem(z + dz + plane_count, plane_count)
        yy = lax.rem(y + dy + Y, Y)
        cc = lax.rem(c + dc, CORES)
        return (zz * Y + yy) * CORES + cc

    return me, z, y, c, hist


def remote(src, dst, send, recv, **device):
    return pltpu.make_async_remote_copy(
        src_ref=src,
        dst_ref=dst,
        send_sem=send,
        recv_sem=recv,
        device_id=device,
        device_id_type=pl.DeviceIdType.MESH,
    )


def greet(partners):
    barrier = pltpu.get_barrier_semaphore()
    for device in partners:
        pl.semaphore_signal(
            barrier, inc=1, device_id=device, device_id_type=pl.DeviceIdType.MESH
        )
    pl.semaphore_wait(barrier, len(partners))


def gather_kernel(
    planes, table_ref, code_ref, out_ref,
    tabs, stage_far, stage_near, far, near, codes, code_words,
    load_sem, ring_send, ring_recv, far_send, far_recv, near_send, near_recv,
    code_send, code_recv, word_sem,
):
    me, z, y, c, hist = place(planes)
    sign = 1 - 2 * c
    half = planes // 2
    tiles = table_ref.shape[0]
    rows = table_ref.shape[2]
    slots = out_ref.shape[0]

    def part(chunk, rel, core, lo=0, n=tiles):
        return tabs[chunk].at[pl.ds((rel * CORES + core) * tiles + lo, n)]

    loads = [
        pltpu.make_async_copy(table_ref.at[:, r], part(r, 0, 0), load_sem.at[r])
        for r in range(CHUNKS)
    ]
    for copy in loads:
        copy.start()

    column = [hist(dz=sign * d) for d in range(1, planes)]
    right, left, partner = hist(dy=1), hist(dy=-1), hist(dc=1)
    ahead, behind = hist(dz=sign), hist(dz=-sign)
    greet([{"hist": d} for d in column + [right, left, partner]])

    own_code = pltpu.make_async_copy(code_ref, codes.at[0], code_recv.at[0])
    own_code.start()
    asks = []
    for d in range(1, planes):
        copy = remote(
            code_ref, codes.at[d], code_send.at[d], code_recv.at[d], hist=column[d - 1]
        )
        copy.start()
        asks.append(copy)

    def ring(chunk, which, src, dst, device):
        return remote(
            src, dst, ring_send.at[chunk, which], ring_recv.at[chunk, which], hist=device
        )

    h = tiles // 2
    moves = []
    for r in range(CHUNKS):
        moves.append([
            ring(r, 0, part(r, 0, 0), part(r, 1, 0), right),
            ring(r, 1, part(r, 0, 0), part(r, 2, 0), left),
            ring(r, 2, part(r, 0, 0), part(r, 0, 1), partner),
            ring(r, 3, part(r, 1, 0, 0, h), part(r, 3, 0, 0, h), right),
            ring(r, 4, part(r, 2, 0, h, h), part(r, 3, 0, h, h), left),
            ring(r, 5, part(r, 1, 0), part(r, 1, 1), partner),
            ring(r, 6, part(r, 2, 0), part(r, 2, 1), partner),
            ring(r, 7, part(r, 3, 0, 0, h), part(r, 3, 1, 0, h), partner),
            ring(r, 8, part(r, 3, 0, h, h), part(r, 3, 1, h, h), partner),
        ])

    def own_out(r):
        loads[r].wait()
        for m in (0, 1, 2):
            moves[r][m].start()

    def pass_on(r):
        moves[r][0].wait_recv()
        moves[r][3].start()
        moves[r][1].wait_recv()
        moves[r][4].start()
        moves[r][5].start()
        moves[r][6].start()

    def across(r):
        moves[r][3].wait_recv()
        moves[r][7].start()
        moves[r][4].wait_recv()
        moves[r][8].start()

    def plane_ready(r):
        for m in (2, 5, 6, 7, 8):
            moves[r][m].wait_recv()

    def fill(r, dst, slot, merge):
        def body(i, carry):
            code = code_words[slot, 0, i]
            tile = tabs[r][lax.rem(code, PLANE * tiles)]
            if merge:
                tile = jnp.where(code // (PLANE * tiles) == z, tile, dst[i])
            dst[i] = tile
            return carry

        lax.fori_loop(0, slots, body, 0)

    far_moves = [
        [
            remote(
                stage_far.at[r] if s == 0 else far.at[r, s - 1], far.at[r, s],
                far_send.at[r, s], far_recv.at[r, s], hist=ahead,
            )
            for s in range(half)
        ]
        for r in range(CHUNKS)
    ]
    near_moves = [
        [
            remote(
                stage_near.at[r] if s == 0 else near.at[r, s - 1], near.at[r, s],
                near_send.at[r, s], near_recv.at[r, s], hist=behind,
            )
            for s in range(half - 1)
        ]
        for r in range(CHUNKS)
    ]

    def step(r, s):
        distance = half - s
        if s == 0:
            fill(r, stage_far.at[r], planes - distance, False)
        else:
            far_moves[r][s - 1].wait_recv()
            fill(r, far.at[r, s - 1], planes - distance, True)
        far_moves[r][s].start()
        if s < half - 1:
            distance = half - 1 - s
            if s == 0:
                fill(r, stage_near.at[r], distance, False)
            else:
                near_moves[r][s - 1].wait_recv()
                fill(r, near.at[r, s - 1], distance, True)
            near_moves[r][s].start()

    def finish(r):
        near_moves[r][half - 2].wait_recv()
        far_moves[r][half - 1].wait_recv()

        def body(i, carry):
            code = code_words[0, 0, i]
            source = code // (PLANE * tiles)
            tile = tabs[r][lax.rem(code, PLANE * tiles)]
            away = lax.rem(sign * (z - source) + planes, planes)
            other = jnp.where(away <= half, far[r, half - 1, i], near[r, half - 2, i])
            out_ref[i, pl.ds(r * rows, rows)] = jnp.where(away == 0, tile, other)
            return carry

        lax.fori_loop(0, slots, body, 0)

    def words():
        own_code.wait()
        for copy in asks:
            copy.wait_recv()
        copy = pltpu.make_async_copy(codes, code_words, word_sem)
        copy.start()
        copy.wait()

    events = [(-9, own_out, (0,)), (-8, words, ()), (-7, pass_on, (0,))]
    for r in range(CHUNKS):
        if r:
            events.append((half * r - half + 0.5, pass_on, (r,)))
            events.append((half * r - half + 2.5, across, (r,)))
        else:
            events.append((-5, across, (r,)))
        if r + 1 < CHUNKS:
            events.append((half * (r - 1) + 0.6 if r else -6, own_out, (r + 1,)))
        events.append((half * r - 0.5, plane_ready, (r,)))
        for s in range(half):
            events.append((half * r + 2 * s + 0.01 * r, step, (r, s)))
        events.append((half * r + 2 * half + 0.7, finish, (r,)))
    for _, act, args in sorted(events, key=lambda e: e[0]):
        act(*args)

    for group in moves + far_moves + near_moves + [asks]:
        for copy in group:
            copy.wait_send()


def pull(planes, table, code):
    tiles, tile_rows, width = table.shape
    slots = tiles
    rows = tile_rows // CHUNKS
    half = planes // 2
    dma = pltpu.SemaphoreType.DMA
    block = (slots, rows, width)
    return pl.pallas_call(
        functools.partial(gather_kernel, planes),
        out_shape=jax.ShapeDtypeStruct((slots, tile_rows, width), table.dtype),
        in_specs=[
            pl.BlockSpec(memory_space=pl.ANY),
            pl.BlockSpec(memory_space=pltpu.VMEM),
        ],
        out_specs=pl.BlockSpec(memory_space=pltpu.VMEM),
        scratch_shapes=[
            [pltpu.VMEM((PLANE * tiles, rows, width), table.dtype)] * CHUNKS,
            pltpu.VMEM((CHUNKS,) + block, table.dtype),
            pltpu.VMEM((CHUNKS,) + block, table.dtype),
            pltpu.VMEM((CHUNKS, half) + block, table.dtype),
            pltpu.VMEM((CHUNKS, half - 1) + block, table.dtype),
            pltpu.VMEM((planes, 8, 128), jnp.int32),
            pltpu.SMEM((planes, 8, 128), jnp.int32),
            dma((CHUNKS,)),
            dma((CHUNKS, 9)),
            dma((CHUNKS, 9)),
            dma((CHUNKS, half)),
            dma((CHUNKS, half)),
            dma((CHUNKS, half - 1)),
            dma((CHUNKS, half - 1)),
            dma((planes,)),
            dma((planes,)),
            dma(()),
        ],
        compiler_params=pltpu.CompilerParams(
            collective_id=0, has_side_effects=True, vmem_limit_bytes=60 << 20
        ),
    )(table.reshape(tiles, CHUNKS, rows, width), code)


GROUPS = 3


def layer_kernel(
    planes, reps, relation_ref, pulled_ref, adjacency_ref, features_ref, cotangent_ref, weights_ref,
    fresh_ref, grad_x_ref, grad_w_ref,
    masked, stacked, pre_ref, dpre_ref, product, kept, give, take,
    to_right, to_left, opposite, half_in, from_left, from_right, mine, z_out, z_in, share,
    pair_send, pair_recv, y_send, y_recv, z_send, z_recv, x_send, x_recv,
):
    me, z, y, c, hist = place(planes)
    x = lax.axis_index("rep")
    blocks, tile, width = pulled_ref.shape
    mats = weights_ref.shape[0]
    relations = mats - 1
    batch_tiles = features_ref.shape[0] // tile
    per_tile = blocks // batch_tiles
    own_rows = width // (planes * PLANE)
    per = mats // GROUPS

    right, left, partner = hist(dy=1), hist(dy=-1), hist(dc=1)
    column = [hist(dz=d) for d in range(1, planes)]
    others = [lax.rem(x + d, reps) for d in range(1, reps)]
    greet(
        [{"hist": d} for d in column + [right, left, partner]] + [{"rep": d} for d in others]
    )

    stacked[0] = features_ref[...]

    def mix(i, carry):
        t, q = i // relations, lax.rem(i, relations)
        for k in range(per_tile):
            hit = relation_ref[0, t * per_tile + k] == q
            block = adjacency_ref[t * per_tile + k]
            masked[:, k * tile:(k + 1) * tile] = jnp.where(hit, block, jnp.zeros_like(block))
        rhs = pulled_ref[pl.ds(t * per_tile, per_tile)].reshape(per_tile * tile, width)
        total = jnp.dot(masked[...], rhs, preferred_element_type=jnp.float32)
        stacked[1 + q, pl.ds(t * tile, tile)] = total.astype(stacked.dtype)
        return carry

    lax.fori_loop(0, batch_tiles * relations, mix, 0)

    pre_ref[...] = jnp.dot(stacked[0], weights_ref[0], preferred_element_type=jnp.float32)

    def project(j, carry):
        pre_ref[...] += jnp.dot(stacked[j], weights_ref[j], preferred_element_type=jnp.float32)
        return carry

    lax.fori_loop(1, mats, project, 0)

    wide_x = features_ref[...].astype(jnp.float32)
    wide_g = cotangent_ref[...].astype(jnp.float32)
    pre = pre_ref[...]
    sigma = jax.nn.sigmoid(pre)
    fresh_ref[...] = (wide_x + pre * sigma).astype(fresh_ref.dtype)
    dpre_ref[...] = (wide_g * sigma * (1.0 + pre * (1.0 - sigma))).astype(dpre_ref.dtype)

    pair = [
        remote(
            give.at[g], take.at[g], pair_send.at[g], pair_recv.at[g], hist=partner
        )
        for g in range(GROUPS)
    ]
    hr = planes * own_rows // 2

    def products(g):
        def one(i, carry):
            value = lax.dot_general(
                stacked[g * per + i], dpre_ref[...], (((0,), (0,)), ((), ())),
                preferred_element_type=jnp.float32,
            )
            product[...] = value.reshape(planes, Y, CORES, own_rows, width)
            for yy in range(Y):
                kept[g, yy, i] = product[:, yy, c].reshape(planes * own_rows, width)
                give[g, yy, i] = product[:, yy, 1 - c].reshape(
                    planes * own_rows, width
                ).astype(give.dtype)
            return carry

        lax.fori_loop(0, per, one, 0)
        pair[g].start()

    top, low = pl.ds(0, hr), pl.ds(hr, hr)

    def turn(g, which, src, dst, device):
        return remote(src, dst, y_send.at[g, which], y_recv.at[g, which], hist=device)

    turns = [
        [
            turn(g, 0, opposite.at[g, :, top], half_in.at[g, :, top], right),
            turn(g, 1, opposite.at[g, :, low], half_in.at[g, :, low], left),
            turn(g, 2, to_right.at[g, :, low], from_left.at[g, :, low], right),
            turn(g, 3, to_left.at[g, :, top], from_right.at[g, :, top], left),
            turn(g, 4, to_right.at[g, :, top], from_left.at[g, :, top], right),
            turn(g, 5, to_left.at[g, :, low], from_right.at[g, :, low], left),
        ]
        for g in range(GROUPS)
    ]
    y_right, y_left, y_far = lax.rem(y + 1, Y), lax.rem(y + Y - 1, Y), lax.rem(y + 2, Y)

    def y_first(g):
        pair[g].wait_recv()
        kind = opposite.dtype

        def one(i, carry):
            opposite[g, i] = (kept[g, y_far, i] + take[g, y_far, i].astype(jnp.float32)).astype(kind)
            right_sum = kept[g, y_right, i] + take[g, y_right, i].astype(jnp.float32)
            left_sum = kept[g, y_left, i] + take[g, y_left, i].astype(jnp.float32)
            to_right[g, i, low] = right_sum[hr:].astype(kind)
            to_left[g, i, top] = left_sum[:hr].astype(kind)
            kept[g, y_right, i] = right_sum
            kept[g, y_left, i] = left_sum
            return carry

        lax.fori_loop(0, per, one, 0)
        for m in range(4):
            turns[g][m].start()

    def y_second(g):
        turns[g][0].wait_recv()
        turns[g][1].wait_recv()

        def one(i, carry):
            up = kept[g, y_right, i, top] + half_in[g, i, top].astype(jnp.float32)
            down = kept[g, y_left, i, low] + half_in[g, i, low].astype(jnp.float32)
            to_right[g, i, top] = up.astype(to_right.dtype)
            to_left[g, i, low] = down.astype(to_left.dtype)
            return carry

        lax.fori_loop(0, per, one, 0)
        turns[g][4].start()
        turns[g][5].start()

    def y_last(g):
        for m in (2, 3, 4, 5):
            turns[g][m].wait_recv()

        def one(i, carry):
            total = kept[g, y, i] + take[g, y, i].astype(jnp.float32)
            total = total + from_left[g, i].astype(jnp.float32)
            total = total + from_right[g, i].astype(jnp.float32)
            mine[:, g * per + i] = total.reshape(planes, own_rows, width)
            return carry

        lax.fori_loop(0, per, one, 0)

    products(0)
    grad_x_ref[...] = (
        wide_g
        + lax.dot_general(
            dpre_ref[...], weights_ref[0], (((1,), (1,)), ((), ())),
            preferred_element_type=jnp.float32,
        )
    ).astype(grad_x_ref.dtype)
    for g in range(1, GROUPS):
        products(g)
        y_first(g - 1)
        if g > 1:
            y_second(g - 2)
    y_first(GROUPS - 1)
    if GROUPS > 1:
        y_second(GROUPS - 2)
    y_second(GROUPS - 1)
    for g in range(GROUPS):
        y_last(g)

    z_rows = mats * own_rows

    def stage_z(p, carry):
        z_out[p, pl.ds(0, z_rows)] = mine[p].reshape(z_rows, width).astype(z_out.dtype)
        return carry

    lax.fori_loop(0, planes, stage_z, 0)
    z_moves = []
    for d in range(1, planes):
        to = lax.rem(z + d, planes)
        copy = remote(
            z_out.at[to], z_in.at[d], z_send.at[d], z_recv.at[d], hist=column[d - 1]
        )
        copy.start()
        z_moves.append(copy)
    total = mine[z].reshape(z_rows, width)
    for d in range(1, planes):
        z_moves[d - 1].wait_recv()
        total = total + z_in[d, pl.ds(0, z_rows)].astype(jnp.float32)

    share[x] = total
    x_moves = []
    for d in range(1, reps):
        copy = remote(
            share.at[x], share.at[x], x_send.at[d], x_recv.at[d], rep=others[d - 1]
        )
        copy.start()
        x_moves.append(copy)
    for copy in x_moves:
        copy.wait_recv()
    total = share[0]
    for d in range(1, reps):
        total = total + share[d]
    grad_w_ref[...] = total.reshape(grad_w_ref.shape)

    for group in [pair, z_moves, x_moves] + turns:
        for copy in group:
            copy.wait_send()


def layer(planes, reps, relation, pulled, tiles, features, cotangent, weights):
    mats, width, _ = weights.shape
    batch = features.shape[0]
    blocks, tile, _ = pulled.shape
    per_tile = blocks * tile // batch
    own_rows = width // (planes * PLANE)
    per = mats // GROUPS
    piece = planes * own_rows
    z_pad = -(-mats * own_rows // 16) * 16
    low, high = features.dtype, jnp.float32
    dma = pltpu.SemaphoreType.DMA
    vmem = pl.BlockSpec(memory_space=pltpu.VMEM)
    return pl.pallas_call(
        functools.partial(layer_kernel, planes, reps),
        out_shape=(
            jax.ShapeDtypeStruct((batch, width), low),
            jax.ShapeDtypeStruct((batch, width), low),
            jax.ShapeDtypeStruct((mats, own_rows, width), high),
        ),
        in_specs=[pl.BlockSpec(memory_space=pltpu.SMEM)] + [vmem] * 5,
        out_specs=(vmem, vmem, vmem),
        scratch_shapes=[
            pltpu.VMEM((tile, per_tile * tile), low),
            pltpu.VMEM((mats, batch, width), low),
            pltpu.VMEM((batch, width), high),
            pltpu.VMEM((batch, width), low),
            pltpu.VMEM((planes, Y, CORES, own_rows, width), high),
            pltpu.VMEM((GROUPS, Y, per, piece, width), high),
            pltpu.VMEM((GROUPS, Y, per, piece, width), low),
            pltpu.VMEM((GROUPS, Y, per, piece, width), low),
            pltpu.VMEM((GROUPS, per, piece, width), low),
            pltpu.VMEM((GROUPS, per, piece, width), low),
            pltpu.VMEM((GROUPS, per, piece, width), low),
            pltpu.VMEM((GROUPS, per, piece, width), low),
            pltpu.VMEM((GROUPS, per, piece, width), low),
            pltpu.VMEM((GROUPS, per, piece, width), low),
            pltpu.VMEM((planes, mats, own_rows, width), high),
            pltpu.VMEM((planes, z_pad, width), low),
            pltpu.VMEM((planes, z_pad, width), low),
            pltpu.VMEM((reps, mats * own_rows, width), high),
            dma((GROUPS,)),
            dma((GROUPS,)),
            dma((GROUPS, 6)),
            dma((GROUPS, 6)),
            dma((planes,)),
            dma((planes,)),
            dma((reps,)),
            dma((reps,)),
        ],
        compiler_params=pltpu.CompilerParams(
            collective_id=1, has_side_effects=True, vmem_limit_bytes=60 << 20
        ),
    )(relation, pulled, tiles, features, cotangent, weights)


def on_device(
    planes, reps, features, history, blk_owner, blk_offset, blk_relation, adjacency, weights, cotangent
):
    owners = blk_owner.reshape(1, -1)
    tiles = adjacency[0]
    tile_rows = tiles.shape[-1]
    width = weights.shape[-1]
    mats = weights.shape[0]
    table = history.reshape(-1, tile_rows, width)

    me = lax.axis_index("hist")
    y, c = (me // CORES) % Y, me % CORES
    away = ((owners // CORES) % Y - y + Y) % Y
    rel = jnp.where(away == 0, 0, jnp.where(away == 3, 1, jnp.where(away == 1, 2, 3)))
    core = jnp.abs(owners % CORES - c)
    spot = (rel * CORES + core) * table.shape[0] + blk_offset.reshape(1, -1)
    code = (owners // PLANE) * (PLANE * table.shape[0]) + spot
    code = jnp.pad(code, ((0, 7), (0, 128 - code.shape[1])))

    pulled = pull(planes, table, code)
    fresh, grad_x, grad_w = layer(
        planes, reps, blk_relation, pulled, tiles, features[0], cotangent[0], weights
    )
    return fresh[None], grad_x[None], grad_w.reshape(mats, -1)


def solution(mesh):
    planes = mesh.shape["hist"] // PLANE
    in_specs = (
        P("rep", "hist", None),
        P("rep", "hist", None),
        P("rep", "hist", None),
        P("rep", "hist"),
        P("rep", "hist"),
        P("rep", "hist", None, None),
        P(),
        P("rep", "hist", None),
    )
    out_specs = (P("rep", "hist", None), P("rep", "hist", None), P(None, "hist"))
    return jax.shard_map(
        functools.partial(on_device, planes, mesh.shape["rep"]),
        mesh=mesh, in_specs=in_specs, out_specs=out_specs, check_vma=False,
    )
```

time: 728 us -> 283 us (0.39)
  waiting for transfers between devices: 603 us -> 0 us
  Pallas kernels: 0 us -> 276 us
  local copies, waits for them, and re-layouts: 52.9 us -> 5.72 us
  matrix products: 24.7 us -> 0 us
  blocking collectives: 20.5 us -> 0 us
  between operations: 14.2 us -> 0.69 us
    all_to_all x1 -> x0, waiting for transfers between devices: 368 us -> none  [on_device(): lax.all_to_all(table[asked], 'hist', split_axis=0, concat_axis=0, tiled=T...]
    pallas_call x0 -> x2, Pallas kernels: none -> 276 us  [the longest x1 206 us: pull(): pl.pallas_call(functools.partial(gather_kernel, planes), out_shape=jax.Sh...]
    reduce_scatter x1 -> x0, waiting for transfers between devices: 188 us -> none  [on_device(): share = lax.psum_scatter(flat_grad, 'hist', scatter_dimension=1, tiled=True)]
    psum x1 -> x0, waiting for transfers between devices: 46.3 us -> none  [on_device(): summed = lax.psum(share, 'rep')]
    unnamed x16 -> x4, local copies, waits for them, and re-layouts: 31.5 us -> 5.13 us
    dot_general x5 -> x0, matrix products: 24.7 us -> none  [the longest x1 9.45 us: on_device(): jnp.einsum('trid,tie->rde', stacked, dpre, preferred_element_type=jnp.flo...]
    all_to_all x1 -> x0, blocking collectives: 20.5 us -> none  [on_device(): lax.all_to_all(request, 'hist', split_axis=0, concat_axis=0, tiled=True)]
    gather x2 -> x0, local copies, waits for them, and re-layouts: 14.2 us -> none  [the longest x1 7.77 us: on_device(): table[asked]]
  transfers between devices with their start and end apart: 3 -> 0, of which waited for: 3 -> 0; matrix products, arithmetic and copies ran while one was open for 1% -> 0% of each run, Pallas kernels for 0% -> 0%
where the time goes in v1:
time: 283 us
  Pallas kernels  276 us (98%)
  local copies, waits for them, and re-layouts  5.72 us (2%)
    pallas_call x1, Pallas kernels, pull(): pl.pallas_call(functools.partial(gather_kernel, planes), out_shape=jax.Sh...  206 us
    pallas_call x1, Pallas kernels, layer(): pl.pallas_call(functools.partial(layer_kernel, planes, reps), out_shape=(...  69.9 us

profile of v1, /device:TPU:8, one launch (start us, length us, event | category | flops | bytes accessed | tf_op | source)
XLA Modules:
  0.0 283.3 jit_solution(12624216735152748802)
XLA Ops:
  0.7 0.7 add_add_fusion
  1.4 0.6 pad.4.code_ref
  2.0 206.2 %shard_map.103.pulled_ref = bf16[16,128,512]{2,1,0:T(8,128)(2,1)} custom-call(bf16[16,4,32,512]{3,2,1,0:T(8,128)(2,1)} %bitcast.27, s32[8,128]{1,0:T(8,128)} %pad.4.code_ref), custom_call_target="tpu_custom_call" | custom-call | tf_op jit(solution)/shard_map/pallas_call | solution.py:230
  208.2 69.9 %shard_map.104 = (bf16[256,512]{1,0:T(8,128)(2,1)}, bf16[256,512]{1,0:T(8,128)(2,1)}, f32[9,8,512]{2,1,0:T(8,128)}) custom-call(s32[1,16]{1,0:T(1,128)} %relation_ref.1, bf16[16,128,512]{2,1,0:T(8,128)(2,1)} %shard_map.103.pulled_ref, bf16[16,128,128]{2,1,0:T(8,128)(2,1)} %bitcast.29, bf16[256,512]{1,0:T(8,128)(2,1)} %bitcast.30, bf16[256,512]{1,0:T(8,128)(2,1)} %bitcast.31, ...), custom_call_target="tpu_custom_call" | custom-call | tf_op jit(solution)/shard_map/pallas_call | solution.py:481
  278.1 0.9 pad.5
  279.1 0.9 copy.11
  279.9 1.7 copy.14
  281.6 1.7 copy.15

commit v2 on v1

--- a/solution.py
+++ b/solution.py
@@ -13,9 +13,13 @@
 CHUNKS = 4
 
 
+def position(index):
+    return lax.div(index, PLANE), lax.rem(lax.div(index, CORES), Y), lax.rem(index, CORES)
+
+
 def place(plane_count):
     me = lax.axis_index("hist")
-    z, y, c = me // PLANE, (me // CORES) % Y, me % CORES
+    z, y, c = position(me)
 
     def hist(dz=0, dy=0, dc=0):
         zz = lax.rem(z + dz + plane_count, plane_count)
@@ -46,11 +50,166 @@
     pl.semaphore_wait(barrier, len(partners))
 
 
+def plane_moves(part, link, tiles, right, left, partner):
+    h = tiles // 2
+    return [
+        link(0, part(0, 0), part(1, 0), right),
+        link(1, part(0, 0), part(2, 0), left),
+        link(2, part(0, 0), part(0, 1), partner),
+        link(3, part(1, 0, 0, h), part(3, 0, 0, h), right),
+        link(4, part(2, 0, h, h), part(3, 0, h, h), left),
+        link(5, part(1, 0), part(1, 1), partner),
+        link(6, part(2, 0), part(2, 1), partner),
+        link(7, part(3, 0, 0, h), part(3, 1, 0, h), partner),
+        link(8, part(3, 0, h, h), part(3, 1, h, h), partner),
+    ]
+
+
+def own_out(moves):
+    for m in (0, 1, 2):
+        moves[m].start()
+
+
+def pass_on(moves):
+    moves[0].wait_recv()
+    moves[3].start()
+    moves[1].wait_recv()
+    moves[4].start()
+    moves[5].start()
+    moves[6].start()
+
+
+def across(moves):
+    moves[3].wait_recv()
+    moves[7].start()
+    moves[4].wait_recv()
+    moves[8].start()
+
+
+def plane_ready(moves):
+    for m in (2, 5, 6, 7, 8):
+        moves[m].wait_recv()
+
+
+def part_of(ref, tiles):
+    def part(rel, core, lo=0, n=tiles):
+        return ref.at[pl.ds((rel * CORES + core) * tiles + lo, n)]
+
+    return part
+
+
+def ask_kernel(
+    planes, reps, table_ref, code_ref, tab_ref, codes, level_ref,
+    flags, plane_flags, rep_flags, own_sem, load_sem, code_send, code_recv,
+    flag_send, flag_recv, top_send, top_recv, ring_send, ring_recv,
+):
+    me, z, y, c, hist = place(planes)
+    sign = 1 - 2 * c
+    x = lax.axis_index("rep")
+    tiles = table_ref.shape[0]
+    part = part_of(tab_ref, tiles)
+    load = pltpu.make_async_copy(table_ref.at[:, 0], part(0, 0), load_sem)
+    load.start()
+    right, left, partner = hist(dy=1), hist(dy=-1), hist(dc=1)
+    column = [hist(dz=sign * d) for d in range(1, planes)]
+    plane = [hist(dy=d // CORES, dc=d % CORES) for d in range(1, PLANE)]
+    others = [lax.rem(x + d, reps) for d in range(1, reps)]
+    greet(
+        [{"hist": d} for d in column + plane] + [{"rep": d} for d in others]
+    )
+
+    own = pltpu.make_async_copy(code_ref, codes.at[0], own_sem)
+    own.start()
+    asks = []
+    for d in range(1, planes):
+        copy = remote(
+            code_ref, codes.at[d], code_send.at[d], code_recv.at[d], hist=column[d - 1]
+        )
+        copy.start()
+        asks.append(copy)
+
+    def link(which, src, dst, device):
+        return remote(src, dst, ring_send.at[which], ring_recv.at[which], hist=device)
+
+    moves = plane_moves(part, link, tiles, right, left, partner)
+    load.wait()
+    own_out(moves)
+
+    own.wait()
+    for copy in asks:
+        copy.wait_recv()
+    top = codes[0]
+    for d in range(1, planes):
+        top = jnp.maximum(top, codes[d])
+    flags[0] = top
+    spread = []
+    for d in range(1, PLANE):
+        copy = remote(
+            flags.at[0], plane_flags.at[d], flag_send.at[d], flag_recv.at[d], hist=plane[d - 1]
+        )
+        copy.start()
+        spread.append(copy)
+    for d in range(1, PLANE):
+        spread[d - 1].wait_recv()
+        top = jnp.maximum(top, plane_flags[d])
+    flags[1] = top
+    over = []
+    for d in range(1, reps):
+        copy = remote(
+            flags.at[1], rep_flags.at[d], top_send.at[d], top_recv.at[d], rep=others[d - 1]
+        )
+        copy.start()
+        over.append(copy)
+    for d in range(1, reps):
+        over[d - 1].wait_recv()
+        top = jnp.maximum(top, rep_flags[d])
+    level_ref[...] = top
+
+    pass_on(moves)
+    across(moves)
+    plane_ready(moves)
+    for group in (asks, spread, over, moves):
+        for copy in group:
+            copy.wait_send()
+
+
+def ask(planes, reps, table, code):
+    tiles, chunks, rows, width = table.shape
+    dma = pltpu.SemaphoreType.DMA
+    vmem = pl.BlockSpec(memory_space=pltpu.VMEM)
+    words = pltpu.VMEM
+    return pl.pallas_call(
+        functools.partial(ask_kernel, planes, reps),
+        out_shape=(
+            jax.ShapeDtypeStruct((PLANE * tiles, rows, width), table.dtype),
+            jax.ShapeDtypeStruct((planes, 8, 128), jnp.int32),
+            jax.ShapeDtypeStruct((8, 128), jnp.int32),
+        ),
+        in_specs=[pl.BlockSpec(memory_space=pl.ANY), vmem],
+        out_specs=(vmem, vmem, vmem),
+        scratch_shapes=[
+            words((2, 8, 128), jnp.int32),
+            words((PLANE, 8, 128), jnp.int32),
+            words((reps, 8, 128), jnp.int32),
+            dma(()),
+            dma(()),
+            dma((planes,)),
+            dma((planes,)),
+            dma((PLANE,)),
+            dma((PLANE,)),
+            dma((reps,)),
+            dma((reps,)),
+            dma((9,)),
+            dma((9,)),
+        ],
+        compiler_params=pltpu.CompilerParams(collective_id=0, has_side_effects=True),
+    )(table, code)
+
+
 def gather_kernel(
-    planes, table_ref, code_ref, out_ref,
-    tabs, stage_far, stage_near, far, near, codes, code_words,
+    planes, far_room, near_room, table_ref, first_ref, codes, out_ref,
+    tabs, stage_far, stage_near, far, near, far_end, near_end,
     load_sem, ring_send, ring_recv, far_send, far_recv, near_send, near_recv,
-    code_send, code_recv, word_sem,
 ):
     me, z, y, c, hist = place(planes)
     sign = 1 - 2 * c
@@ -59,121 +218,75 @@
     rows = table_ref.shape[2]
     slots = out_ref.shape[0]
 
-    def part(chunk, rel, core, lo=0, n=tiles):
-        return tabs[chunk].at[pl.ds((rel * CORES + core) * tiles + lo, n)]
-
-    loads = [
-        pltpu.make_async_copy(table_ref.at[:, r], part(r, 0, 0), load_sem.at[r])
-        for r in range(CHUNKS)
+    loads = [pltpu.make_async_copy(first_ref, tabs[0], load_sem.at[0])] + [
+        pltpu.make_async_copy(
+            table_ref.at[:, r], tabs[r].at[pl.ds(0, tiles)], load_sem.at[r]
+        )
+        for r in range(1, CHUNKS)
     ]
     for copy in loads:
         copy.start()
 
-    column = [hist(dz=sign * d) for d in range(1, planes)]
     right, left, partner = hist(dy=1), hist(dy=-1), hist(dc=1)
     ahead, behind = hist(dz=sign), hist(dz=-sign)
-    greet([{"hist": d} for d in column + [right, left, partner]])
-
-    own_code = pltpu.make_async_copy(code_ref, codes.at[0], code_recv.at[0])
-    own_code.start()
-    asks = []
-    for d in range(1, planes):
-        copy = remote(
-            code_ref, codes.at[d], code_send.at[d], code_recv.at[d], hist=column[d - 1]
-        )
-        copy.start()
-        asks.append(copy)
-
-    def ring(chunk, which, src, dst, device):
-        return remote(
-            src, dst, ring_send.at[chunk, which], ring_recv.at[chunk, which], hist=device
-        )
-
-    h = tiles // 2
-    moves = []
-    for r in range(CHUNKS):
-        moves.append([
-            ring(r, 0, part(r, 0, 0), part(r, 1, 0), right),
-            ring(r, 1, part(r, 0, 0), part(r, 2, 0), left),
-            ring(r, 2, part(r, 0, 0), part(r, 0, 1), partner),
-            ring(r, 3, part(r, 1, 0, 0, h), part(r, 3, 0, 0, h), right),
-            ring(r, 4, part(r, 2, 0, h, h), part(r, 3, 0, h, h), left),
-            ring(r, 5, part(r, 1, 0), part(r, 1, 1), partner),
-            ring(r, 6, part(r, 2, 0), part(r, 2, 1), partner),
-            ring(r, 7, part(r, 3, 0, 0, h), part(r, 3, 1, 0, h), partner),
-            ring(r, 8, part(r, 3, 0, h, h), part(r, 3, 1, h, h), partner),
-        ])
-
-    def own_out(r):
+    greet([{"hist": d} for d in (right, left, partner, ahead, behind)])
+
+    moves = [[]]
+    for r in range(1, CHUNKS):
+        def link(which, src, dst, device, r=r):
+            return remote(
+                src, dst, ring_send.at[r, which], ring_recv.at[r, which], hist=device
+            )
+
+        moves.append(plane_moves(part_of(tabs[r], tiles), link, tiles, right, left, partner))
+
+    def begin(r):
         loads[r].wait()
-        for m in (0, 1, 2):
-            moves[r][m].start()
-
-    def pass_on(r):
-        moves[r][0].wait_recv()
-        moves[r][3].start()
-        moves[r][1].wait_recv()
-        moves[r][4].start()
-        moves[r][5].start()
-        moves[r][6].start()
-
-    def across(r):
-        moves[r][3].wait_recv()
-        moves[r][7].start()
-        moves[r][4].wait_recv()
-        moves[r][8].start()
-
-    def plane_ready(r):
-        for m in (2, 5, 6, 7, 8):
-            moves[r][m].wait_recv()
-
-    def fill(r, dst, slot, merge):
+        own_out(moves[r])
+
+    def fill(r, dst, slot, lane, count, merge):
         def body(i, carry):
-            code = code_words[slot, 0, i]
+            code = codes[slot, lane, i]
             tile = tabs[r][lax.rem(code, PLANE * tiles)]
             if merge:
-                tile = jnp.where(code // (PLANE * tiles) == z, tile, dst[i])
+                tile = jnp.where(lax.div(code, PLANE * tiles) == z, tile, dst[i])
             dst[i] = tile
             return carry
 
-        lax.fori_loop(0, slots, body, 0)
-
-    far_moves = [
-        [
-            remote(
-                stage_far.at[r] if s == 0 else far.at[r, s - 1], far.at[r, s],
-                far_send.at[r, s], far_recv.at[r, s], hist=ahead,
-            )
-            for s in range(half)
-        ]
-        for r in range(CHUNKS)
-    ]
-    near_moves = [
-        [
-            remote(
-                stage_near.at[r] if s == 0 else near.at[r, s - 1], near.at[r, s],
-                near_send.at[r, s], near_recv.at[r, s], hist=behind,
-            )
-            for s in range(half - 1)
-        ]
-        for r in range(CHUNKS)
-    ]
+        lax.fori_loop(0, count, body, 0, unroll=2)
+
+    def chain(stage, middle, end, room, send, recv, device):
+        last = len(room) - 1
+        ready = []
+        for r in range(CHUNKS):
+            hops = []
+            for s, count in enumerate(room):
+                src = stage.at[r] if s == 0 else middle.at[r, s - 1]
+                dst = end[r] if s == last else middle.at[r, s]
+                some = pl.ds(0, count)
+                hops.append(
+                    remote(src.at[some], dst.at[some], send.at[r, s], recv.at[r, s], hist=device)
+                )
+            ready.append(hops)
+        return ready
+
+    far_moves = chain(stage_far, far, far_end, far_room, far_send, far_recv, ahead)
+    near_moves = chain(stage_near, near, near_end, near_room, near_send, near_recv, behind)
 
     def step(r, s):
-        distance = half - s
         if s == 0:
-            fill(r, stage_far.at[r], planes - distance, False)
+            fill(r, stage_far.at[r], planes - half, 0, far_room[0], False)
         else:
             far_moves[r][s - 1].wait_recv()
-            fill(r, far.at[r, s - 1], planes - distance, True)
+            fill(r, far.at[r, s - 1], planes - half + s, 0, far_room[s], True)
         far_moves[r][s].start()
         if s < half - 1:
             distance = half - 1 - s
             if s == 0:
-                fill(r, stage_near.at[r], distance, False)
+                fill(r, stage_near.at[r], distance, 1, near_room[0], False)
             else:
                 near_moves[r][s - 1].wait_recv()
-                fill(r, near.at[r, s - 1], distance, True)
+                fill(r, near.at[r, s - 1], distance, 1, near_room[s], True)
             near_moves[r][s].start()
 
     def finish(r):
@@ -181,83 +294,117 @@
         far_moves[r][half - 1].wait_recv()
 
         def body(i, carry):
-            code = code_words[0, 0, i]
-            source = code // (PLANE * tiles)
-            tile = tabs[r][lax.rem(code, PLANE * tiles)]
-            away = lax.rem(sign * (z - source) + planes, planes)
-            other = jnp.where(away <= half, far[r, half - 1, i], near[r, half - 2, i])
-            out_ref[i, pl.ds(r * rows, rows)] = jnp.where(away == 0, tile, other)
+            kind = codes[0, 2, i]
+            spot = codes[0, 3, i]
+            tile = tabs[r][codes[0, 4, i]]
+            other = jnp.where(kind == 1, far_end[r][spot], near_end[r][spot])
+            out_ref[i, pl.ds(r * rows, rows)] = jnp.where(kind == 0, tile, other)
             return carry
 
-        lax.fori_loop(0, slots, body, 0)
-
-    def words():
-        own_code.wait()
-        for copy in asks:
-            copy.wait_recv()
-        copy = pltpu.make_async_copy(codes, code_words, word_sem)
-        copy.start()
-        copy.wait()
-
-    events = [(-9, own_out, (0,)), (-8, words, ()), (-7, pass_on, (0,))]
+        lax.fori_loop(0, slots, body, 0, unroll=2)
+
+    def first():
+        loads[0].wait()
+
+    events = [(-9, first, ())]
     for r in range(CHUNKS):
         if r:
-            events.append((half * r - half + 0.5, pass_on, (r,)))
-            events.append((half * r - half + 2.5, across, (r,)))
-        else:
-            events.append((-5, across, (r,)))
+            events.append((half * r - half + 0.5, pass_on, (moves[r],)))
+            events.append((half * r - half + 2.5, across, (moves[r],)))
+            events.append((half * r - 0.5, plane_ready, (moves[r],)))
         if r + 1 < CHUNKS:
-            events.append((half * (r - 1) + 0.6 if r else -6, own_out, (r + 1,)))
-        events.append((half * r - 0.5, plane_ready, (r,)))
+            events.append((half * (r - 1) + 0.6 if r else -8, begin, (r + 1,)))
         for s in range(half):
             events.append((half * r + 2 * s + 0.01 * r, step, (r, s)))
         events.append((half * r + 2 * half + 0.7, finish, (r,)))
     for _, act, args in sorted(events, key=lambda e: e[0]):
         act(*args)
 
-    for group in moves + far_moves + near_moves + [asks]:
+    for group in moves + far_moves + near_moves:
         for copy in group:
             copy.wait_send()
 
 
-def pull(planes, table, code):
-    tiles, tile_rows, width = table.shape
+def pull(planes, level, far_room, near_room, table, first, codes):
+    tiles, chunks, rows, width = table.shape
     slots = tiles
-    rows = tile_rows // CHUNKS
     half = planes // 2
     dma = pltpu.SemaphoreType.DMA
     block = (slots, rows, width)
+    hbm = pl.BlockSpec(memory_space=pl.ANY)
     return pl.pallas_call(
-        functools.partial(gather_kernel, planes),
-        out_shape=jax.ShapeDtypeStruct((slots, tile_rows, width), table.dtype),
-        in_specs=[
-            pl.BlockSpec(memory_space=pl.ANY),
-            pl.BlockSpec(memory_space=pltpu.VMEM),
-        ],
+        functools.partial(gather_kernel, planes, far_room, near_room),
+        out_shape=jax.ShapeDtypeStruct((slots, chunks * rows, width), table.dtype),
+        in_specs=[hbm, hbm, pl.BlockSpec(memory_space=pltpu.SMEM)],
         out_specs=pl.BlockSpec(memory_space=pltpu.VMEM),
         scratch_shapes=[
-            [pltpu.VMEM((PLANE * tiles, rows, width), table.dtype)] * CHUNKS,
-            pltpu.VMEM((CHUNKS,) + block, table.dtype),
-            pltpu.VMEM((CHUNKS,) + block, table.dtype),
-            pltpu.VMEM((CHUNKS, half) + block, table.dtype),
-            pltpu.VMEM((CHUNKS, half - 1) + block, table.dtype),
-            pltpu.VMEM((planes, 8, 128), jnp.int32),
-            pltpu.SMEM((planes, 8, 128), jnp.int32),
-            dma((CHUNKS,)),
-            dma((CHUNKS, 9)),
-            dma((CHUNKS, 9)),
-            dma((CHUNKS, half)),
-            dma((CHUNKS, half)),
-            dma((CHUNKS, half - 1)),
-            dma((CHUNKS, half - 1)),
-            dma((planes,)),
-            dma((planes,)),
-            dma(()),
+            [pltpu.VMEM((PLANE * tiles, rows, width), table.dtype)] * chunks,
+            pltpu.VMEM((chunks,) + block, table.dtype),
+            pltpu.VMEM((chunks,) + block, table.dtype),
+            pltpu.VMEM((chunks, half - 1) + block, table.dtype),
+            pltpu.VMEM((chunks, half - 2) + block, table.dtype),
+            [pltpu.VMEM(block, table.dtype)] * chunks,
+            [pltpu.VMEM(block, table.dtype)] * chunks,
+            dma((chunks,)),
+            dma((chunks, 9)),
+            dma((chunks, 9)),
+            dma((chunks, half)),
+            dma((chunks, half)),
+            dma((chunks, half - 1)),
+            dma((chunks, half - 1)),
         ],
         compiler_params=pltpu.CompilerParams(
-            collective_id=0, has_side_effects=True, vmem_limit_bytes=60 << 20
+            collective_id=2 + level, has_side_effects=True, vmem_limit_bytes=60 << 20
         ),
-    )(table.reshape(tiles, CHUNKS, rows, width), code)
+    )(table, first, codes)
+
+
+def rooms(planes, slots):
+    half = planes // 2
+    full = ((slots,) * half, (slots,) * (half - 1))
+    if (planes, slots) != (8, 16):
+        return [full]
+    return [
+        ((6, 9, 11, 13), (6, 9, 11)),
+        ((8, 12, 14, 15), (8, 12, 14)),
+        full,
+    ]
+
+
+def requests(planes, levels, tiles, owners, offsets):
+    me = lax.axis_index("hist")
+    z, y, c = position(me)
+    oz, oy, oc = position(owners)
+    half = planes // 2
+    slots = owners.shape[0]
+    sign = 1 - 2 * c
+    turn = lax.rem(oy - y + Y, Y)
+    rel = jnp.where(turn == 0, 0, jnp.where(turn == 3, 1, jnp.where(turn == 1, 2, 3)))
+    tile = (rel * CORES + jnp.abs(oc - c)) * tiles + offsets
+    code = oz * (PLANE * tiles) + tile
+    away = lax.rem(sign * (z - oz) + planes, planes)
+    place = jnp.arange(slots)
+    far = (away >= 1) & (away <= half)
+    near = away > half
+    keys = jnp.stack([jnp.where(far, half - away, planes), jnp.where(near, away, 2 * planes)])
+    keys = keys * slots + place
+    rank = jnp.sum((keys[:, None, :] < keys[:, :, None]).astype(jnp.int32), axis=2)
+    hit = rank[:, :, None] == place
+    ordered = jnp.sum(jnp.where(hit, code[None, :, None], 0), axis=1)
+    kind = jnp.where(far, 1, jnp.where(near, 2, 0))
+    spot = jnp.where(far, rank[0], rank[1])
+    level = jnp.int32(0)
+    for far_room, near_room in levels[:-1]:
+        over = jnp.bool_(False)
+        for s, room in enumerate(far_room):
+            over |= jnp.sum((far & (away >= half - s)).astype(jnp.int32)) > room
+        for s, room in enumerate(near_room):
+            over |= jnp.sum((near & (away <= half + 1 + s)).astype(jnp.int32)) > room
+        level = level + over.astype(jnp.int32)
+    words = jnp.concatenate(
+        [ordered, jnp.stack([kind, spot, tile, jnp.broadcast_to(level, (slots,))])]
+    )
+    return jnp.pad(words, ((0, 2), (0, 128 - slots)))
 
 
 GROUPS = 3
@@ -290,7 +437,7 @@
     stacked[0] = features_ref[...]
 
     def mix(i, carry):
-        t, q = i // relations, lax.rem(i, relations)
+        t, q = lax.div(i, relations), lax.rem(i, relations)
         for k in range(per_tile):
             hit = relation_ref[0, t * per_tile + k] == q
             block = adjacency_ref[t * per_tile + k]
@@ -524,23 +671,26 @@
 def on_device(
     planes, reps, features, history, blk_owner, blk_offset, blk_relation, adjacency, weights, cotangent
 ):
-    owners = blk_owner.reshape(1, -1)
+    owners = blk_owner.reshape(-1)
     tiles = adjacency[0]
     tile_rows = tiles.shape[-1]
     width = weights.shape[-1]
     mats = weights.shape[0]
     table = history.reshape(-1, tile_rows, width)
 
-    me = lax.axis_index("hist")
-    y, c = (me // CORES) % Y, me % CORES
-    away = ((owners // CORES) % Y - y + Y) % Y
-    rel = jnp.where(away == 0, 0, jnp.where(away == 3, 1, jnp.where(away == 1, 2, 3)))
-    core = jnp.abs(owners % CORES - c)
-    spot = (rel * CORES + core) * table.shape[0] + blk_offset.reshape(1, -1)
-    code = (owners // PLANE) * (PLANE * table.shape[0]) + spot
-    code = jnp.pad(code, ((0, 7), (0, 128 - code.shape[1])))
-
-    pulled = pull(planes, table, code)
+    tiles_held = table.shape[0]
+    table = table.reshape(tiles_held, CHUNKS, tile_rows // CHUNKS, width)
+    levels = rooms(planes, owners.shape[0])
+    words = requests(planes, levels, tiles_held, owners, blk_offset.reshape(-1))
+    first, codes, top = ask(planes, reps, table, words)
+    pulled = lax.switch(
+        top[5, 0],
+        [
+            functools.partial(pull, planes, level, far_room, near_room)
+            for level, (far_room, near_room) in enumerate(levels)
+        ],
+        table, first, codes,
+    )
     fresh, grad_x, grad_w = layer(
         planes, reps, blk_relation, pulled, tiles, features[0], cotangent[0], weights
     )

time: 283 us -> 272 us (0.961); the launches traced: 283 us -> 269 us
  Pallas kernels: 276 us -> 249 us
  between operations: 0.69 us -> 10.3 us
    pallas_call x1 -> x2, Pallas kernels: 206 us -> 182 us  [the longest x1 144 us: pull(): pl.pallas_call(functools.partial(gather_kernel, planes, far_room, near_ro...]
    pallas_call x1, Pallas kernels: 69.9 us -> 66.4 us  [layer(): pl.pallas_call(functools.partial(layer_kernel, planes, reps), out_shape=(...]
where the time goes in v2:
time: 272 us; the launch traced here: 269 us
  Pallas kernels  249 us (92%)
  between operations  10.3 us (4%)
  local copies, waits for them, and re-layouts  6.96 us (3%)
  other arithmetic  3.33 us (1%)
    pallas_call x1, Pallas kernels, pull(): pl.pallas_call(functools.partial(gather_kernel, planes, far_room, near_ro...  144 us
    pallas_call x1, Pallas kernels, layer(): pl.pallas_call(functools.partial(layer_kernel, planes, reps), out_shape=(...  66.4 us
    pallas_call x1, Pallas kernels, ask(): pl.pallas_call(functools.partial(ask_kernel, planes, reps), out_shape=(ja...  37.9 us

profile of v2, /device:TPU:8, one launch (start us, length us, event | category | flops | bytes accessed | tf_op | source)
XLA Modules:
  0.0 269.2 jit_solution(16606903412359307654)
XLA Ops:
  0.6 0.0 copy-start
  0.7 0.8 fusion.17
  1.5 0.7 fusion.31
  2.2 0.2 convert_reduce_fusion
  2.4 0.1 select_reduce_fusion
  2.5 1.5 fusion.15
  13.0 0.6 pad.4.code_ref
  13.6 37.9 %shard_map.103 = (bf16[128,32,512]{2,1,0:T(8,128)(2,1)}, s32[8,8,128]{2,1,0:T(8,128)S(1)}, s32[8,128]{1,0:T(8,128)}) custom-call(bf16[16,4,32,512]{3,2,1,0:T(8,128)(2,1)} %bitcast.40, s32[8,128]{1,0:T(8,128)} %pad.4.code_ref), custom_call_target="tpu_custom_call" | custom-call | tf_op jit(solution)/shard_map/pallas_call | solution.py:181
  51.5 1.2 slice.11
  53.3 0.0 copy-done
  53.3 144.4 %conditional.1 = (bf16[16,128,512]{2,1,0:T(8,128)(2,1)}) conditional(s32[]{:T(128)} %bitcast.7, (bf16[16,4,32,512]{3,2,1,0:T(8,128)(2,1)S(1)}, bf16[128,32,512]{2,1,0:T(8,128)(2,1)}, s32[8,8,128]{2,1,0:T(8,128)S(1)}) %tuple.36, (bf16[16,4,32,512]{3,2,1,0:T(8,128)(2,1)S(1)}, bf16[128,32,512]{2,1,0:T(8,128)(2,1)}, ...), branch_computations={%region_9.10_spmd, %region_10.11_spmd, %region_11.12_spmd} | conditional | bytes 8 | solution.py:686
  53.3 144.4 %branch_1_fun.1 = bf16[16,128,512]{2,1,0:T(8,128)(2,1)} custom-call(bf16[16,4,32,512]{3,2,1,0:T(8,128)(2,1)S(1)} %get-tuple-element.25.table_ref, bf16[128,32,512]{2,1,0:T(8,128)(2,1)} %get-tuple-element.26.first_ref, s32[8,8,128]{2,1,0:T(8,128)S(1)} %get-tuple-element.27.codes), custom_call_target="tpu_custom_call" | custom-call | tf_op jit(solution)/shard_map/cond/branch_1_fun/pallas_call | solution.py:335
  197.7 66.4 %shard_map.104 = (bf16[256,512]{1,0:T(8,128)(2,1)}, bf16[256,512]{1,0:T(8,128)(2,1)}, f32[9,8,512]{2,1,0:T(8,128)}) custom-call(s32[1,16]{1,0:T(1,128)} %relation_ref.1, bf16[16,128,512]{2,1,0:T(8,128)(2,1)} %get-tuple-element.69.pulled_ref, bf16[16,128,128]{2,1,0:T(8,128)(2,1)} %bitcast.45, bf16[256,512]{1,0:T(8,128)(2,1)} %bitcast.46, ...), custom_call_target="tpu_custom_call" | custom-call | tf_op jit(solution)/shard_map/pallas_call | solution.py:628
  264.1 0.9 pad.9
  265.0 0.9 copy.11
  265.9 1.7 copy.17
  267.6 1.7 copy.18
  (6 shorter events, 0.1 us)
Async XLA Ops:
  0.6 52.7 %copy-start = (bf16[1,2048,512]{2,1,0:T(8,128)(2,1)S(1)}, bf16[1,2048,512]{2,1,0:T(8,128)(2,1)}, u32[]{:S(2)}) copy-start(bf16[1,2048,512]{2,1,0:T(8,128)(2,1)} %param.12) | copy-start | bytes 6291460

commit v3 on v2

--- a/solution.py
+++ b/solution.py
@@ -10,7 +10,8 @@
 Y = 4
 CORES = 2
 PLANE = Y * CORES
-CHUNKS = 4
+CHUNKS = 8
+STRIDE = 3
 
 
 def position(index):
@@ -149,6 +150,7 @@
         )
         copy.start()
         spread.append(copy)
+    pass_on(moves)
     for d in range(1, PLANE):
         spread[d - 1].wait_recv()
         top = jnp.maximum(top, plane_flags[d])
@@ -160,13 +162,12 @@
         )
         copy.start()
         over.append(copy)
+    across(moves)
     for d in range(1, reps):
         over[d - 1].wait_recv()
         top = jnp.maximum(top, rep_flags[d])
     level_ref[...] = top
 
-    pass_on(moves)
-    across(moves)
     plane_ready(moves)
     for group in (asks, spread, over, moves):
         for copy in group:
@@ -309,14 +310,14 @@
     events = [(-9, first, ())]
     for r in range(CHUNKS):
         if r:
-            events.append((half * r - half + 0.5, pass_on, (moves[r],)))
-            events.append((half * r - half + 2.5, across, (moves[r],)))
+            events.append((half * (r - 1) + 0.5, pass_on, (moves[r],)))
+            events.append((half * (r - 1) + 2.5, across, (moves[r],)))
             events.append((half * r - 0.5, plane_ready, (moves[r],)))
         if r + 1 < CHUNKS:
             events.append((half * (r - 1) + 0.6 if r else -8, begin, (r + 1,)))
         for s in range(half):
-            events.append((half * r + 2 * s + 0.01 * r, step, (r, s)))
-        events.append((half * r + 2 * half + 0.7, finish, (r,)))
+            events.append((half * r + STRIDE * s + 0.01 * r, step, (r, s)))
+        events.append((half * r + STRIDE * half + 0.7, finish, (r,)))
     for _, act, args in sorted(events, key=lambda e: e[0]):
         act(*args)
 
@@ -366,45 +367,84 @@
         return [full]
     return [
         ((6, 9, 11, 13), (6, 9, 11)),
-        ((8, 12, 14, 15), (8, 12, 14)),
+        ((7, 10, 12, 14), (7, 10, 12)),
+        ((9, 12, 14, 15), (9, 12, 14)),
         full,
     ]
 
 
+def words_kernel(planes, levels, tiles, owner_ref, offset_ref, words, count, start):
+    me, z, y, c, hist = place(planes)
+    sign = 1 - 2 * c
+    half = planes // 2
+    slots = offset_ref.shape[1]
+
+    def parse(k):
+        owner = owner_ref[k, 0]
+        oz, oy, oc = position(owner)
+        turn = lax.rem(oy - y + Y, Y)
+        rel = jnp.where(turn == 0, 0, jnp.where(turn == 3, 1, jnp.where(turn == 1, 2, 3)))
+        tile = (rel * CORES + jnp.abs(oc - c)) * tiles + offset_ref[0, k]
+        away = lax.rem(sign * (z - oz) + planes, planes)
+        return oz * (PLANE * tiles) + tile, tile, away
+
+    any_code = parse(0)[0]
+    for away in range(planes):
+        count[away] = 0
+
+    def tally(k, carry):
+        away = parse(k)[2]
+        count[away] += 1
+        words[0, k] = any_code
+        words[1, k] = any_code
+        return carry
+
+    lax.fori_loop(0, slots, tally, 0)
+
+    far_order = list(range(half, 0, -1))
+    near_order = list(range(half + 1, planes))
+    level = jnp.int32(0)
+    start[0] = 0
+    sums = []
+    for order in (far_order, near_order):
+        total = jnp.int32(0)
+        ends = []
+        for away in order:
+            start[away] = total
+            total = total + count[away]
+            ends.append(total)
+        sums.append(ends)
+    for room in levels[:-1]:
+        over = jnp.int32(0)
+        for ends, caps in zip(sums, room):
+            for end, cap in zip(ends, caps):
+                over = jnp.maximum(over, jnp.where(end > cap, 1, 0))
+        level = level + over
+    words[5, 0] = level
+
+    def put(k, carry):
+        code, tile, away = parse(k)
+        spot = start[away]
+        start[away] = spot + 1
+        kind = jnp.where(away == 0, 0, jnp.where(away <= half, 1, 2))
+        words[jnp.where(kind == 0, 6, kind - 1), spot] = code
+        words[2, k] = kind
+        words[3, k] = jnp.where(kind == 0, 0, spot)
+        words[4, k] = tile
+        return carry
+
+    lax.fori_loop(0, slots, put, 0)
+
+
 def requests(planes, levels, tiles, owners, offsets):
-    me = lax.axis_index("hist")
-    z, y, c = position(me)
-    oz, oy, oc = position(owners)
-    half = planes // 2
-    slots = owners.shape[0]
-    sign = 1 - 2 * c
-    turn = lax.rem(oy - y + Y, Y)
-    rel = jnp.where(turn == 0, 0, jnp.where(turn == 3, 1, jnp.where(turn == 1, 2, 3)))
-    tile = (rel * CORES + jnp.abs(oc - c)) * tiles + offsets
-    code = oz * (PLANE * tiles) + tile
-    away = lax.rem(sign * (z - oz) + planes, planes)
-    place = jnp.arange(slots)
-    far = (away >= 1) & (away <= half)
-    near = away > half
-    keys = jnp.stack([jnp.where(far, half - away, planes), jnp.where(near, away, 2 * planes)])
-    keys = keys * slots + place
-    rank = jnp.sum((keys[:, None, :] < keys[:, :, None]).astype(jnp.int32), axis=2)
-    hit = rank[:, :, None] == place
-    ordered = jnp.sum(jnp.where(hit, code[None, :, None], 0), axis=1)
-    kind = jnp.where(far, 1, jnp.where(near, 2, 0))
-    spot = jnp.where(far, rank[0], rank[1])
-    level = jnp.int32(0)
-    for far_room, near_room in levels[:-1]:
-        over = jnp.bool_(False)
-        for s, room in enumerate(far_room):
-            over |= jnp.sum((far & (away >= half - s)).astype(jnp.int32)) > room
-        for s, room in enumerate(near_room):
-            over |= jnp.sum((near & (away <= half + 1 + s)).astype(jnp.int32)) > room
-        level = level + over.astype(jnp.int32)
-    words = jnp.concatenate(
-        [ordered, jnp.stack([kind, spot, tile, jnp.broadcast_to(level, (slots,))])]
-    )
-    return jnp.pad(words, ((0, 2), (0, 128 - slots)))
+    smem = pl.BlockSpec(memory_space=pltpu.SMEM)
+    return pl.pallas_call(
+        functools.partial(words_kernel, planes, levels, tiles),
+        out_shape=jax.ShapeDtypeStruct((8, 128), jnp.int32),
+        in_specs=[smem, smem],
+        out_specs=smem,
+        scratch_shapes=[pltpu.SMEM((planes,), jnp.int32), pltpu.SMEM((planes,), jnp.int32)],
+    )(owners, offsets)
 
 
 GROUPS = 3
@@ -413,9 +453,10 @@
 def layer_kernel(
     planes, reps, relation_ref, pulled_ref, adjacency_ref, features_ref, cotangent_ref, weights_ref,
     fresh_ref, grad_x_ref, grad_w_ref,
-    masked, stacked, pre_ref, dpre_ref, product, kept, give, take,
-    to_right, to_left, opposite, half_in, from_left, from_right, mine, z_out, z_in, share,
-    pair_send, pair_recv, y_send, y_recv, z_send, z_recv, x_send, x_recv,
+    masked, stacked, pre_ref, dpre_ref, product, kept, give, take, y_bufs, x_bufs, y_sum, x_sum,
+    x_out, x_in, y_out, y_in, mine, z_out, z_in, share,
+    pair_send, pair_recv, y_send, y_recv, x_send, x_recv,
+    x_put, x_get, y_put, y_get, z_send, z_recv, share_send, share_recv,
 ):
     me, z, y, c, hist = place(planes)
     x = lax.axis_index("rep")
@@ -426,157 +467,235 @@
     per_tile = blocks // batch_tiles
     own_rows = width // (planes * PLANE)
     per = mats // GROUPS
+    lanes = width // reps
+    piece = planes * own_rows
+    hp = piece // 2
+    low, high = dpre_ref.dtype, jnp.float32
 
     right, left, partner = hist(dy=1), hist(dy=-1), hist(dc=1)
     column = [hist(dz=d) for d in range(1, planes)]
+    ring = [hist(dy=d) for d in range(1, Y)]
     others = [lax.rem(x + d, reps) for d in range(1, reps)]
     greet(
-        [{"hist": d} for d in column + [right, left, partner]] + [{"rep": d} for d in others]
+        [{"hist": d} for d in column + ring + [partner]] + [{"rep": d} for d in others]
     )
 
     stacked[0] = features_ref[...]
+    pack = 2
 
     def mix(i, carry):
-        t, q = lax.div(i, relations), lax.rem(i, relations)
+        t, q0 = lax.div(i, relations // pack), lax.rem(i, relations // pack) * pack
         for k in range(per_tile):
-            hit = relation_ref[0, t * per_tile + k] == q
+            relation = relation_ref[0, t * per_tile + k]
             block = adjacency_ref[t * per_tile + k]
-            masked[:, k * tile:(k + 1) * tile] = jnp.where(hit, block, jnp.zeros_like(block))
+            for p in range(pack):
+                masked[p * tile:(p + 1) * tile, k * tile:(k + 1) * tile] = jnp.where(
+                    relation == q0 + p, block, jnp.zeros_like(block)
+                )
         rhs = pulled_ref[pl.ds(t * per_tile, per_tile)].reshape(per_tile * tile, width)
-        total = jnp.dot(masked[...], rhs, preferred_element_type=jnp.float32)
-        stacked[1 + q, pl.ds(t * tile, tile)] = total.astype(stacked.dtype)
+        total = jnp.dot(masked[...], rhs, preferred_element_type=high).astype(low)
+        for p in range(pack):
+            stacked[1 + q0 + p, pl.ds(t * tile, tile)] = total[p * tile:(p + 1) * tile]
         return carry
 
-    lax.fori_loop(0, batch_tiles * relations, mix, 0)
-
-    pre_ref[...] = jnp.dot(stacked[0], weights_ref[0], preferred_element_type=jnp.float32)
+    lax.fori_loop(0, batch_tiles * relations // pack, mix, 0)
+
+    pre_ref[...] = jnp.dot(stacked[0], weights_ref[0], preferred_element_type=high)
 
     def project(j, carry):
-        pre_ref[...] += jnp.dot(stacked[j], weights_ref[j], preferred_element_type=jnp.float32)
+        pre_ref[...] += jnp.dot(stacked[j], weights_ref[j], preferred_element_type=high)
         return carry
 
     lax.fori_loop(1, mats, project, 0)
 
-    wide_x = features_ref[...].astype(jnp.float32)
-    wide_g = cotangent_ref[...].astype(jnp.float32)
+    wide_x = features_ref[...].astype(high)
+    wide_g = cotangent_ref[...].astype(high)
     pre = pre_ref[...]
     sigma = jax.nn.sigmoid(pre)
     fresh_ref[...] = (wide_x + pre * sigma).astype(fresh_ref.dtype)
-    dpre_ref[...] = (wide_g * sigma * (1.0 + pre * (1.0 - sigma))).astype(dpre_ref.dtype)
+    dpre_ref[...] = (wide_g * sigma * (1.0 + pre * (1.0 - sigma))).astype(low)
 
     pair = [
-        remote(
-            give.at[g], take.at[g], pair_send.at[g], pair_recv.at[g], hist=partner
-        )
+        remote(give.at[g], take.at[g], pair_send.at[g], pair_recv.at[g], hist=partner)
         for g in range(GROUPS)
     ]
-    hr = planes * own_rows // 2
 
     def products(g):
         def one(i, carry):
             value = lax.dot_general(
                 stacked[g * per + i], dpre_ref[...], (((0,), (0,)), ((), ())),
-                preferred_element_type=jnp.float32,
+                preferred_element_type=high,
             )
             product[...] = value.reshape(planes, Y, CORES, own_rows, width)
             for yy in range(Y):
-                kept[g, yy, i] = product[:, yy, c].reshape(planes * own_rows, width)
-                give[g, yy, i] = product[:, yy, 1 - c].reshape(
-                    planes * own_rows, width
-                ).astype(give.dtype)
+                kept[g, yy, i] = product[:, yy, c].reshape(piece, width)
+                give[g, yy, i] = product[:, yy, 1 - c].reshape(piece, width).astype(low)
             return carry
 
         lax.fori_loop(0, per, one, 0)
         pair[g].start()
 
-    top, low = pl.ds(0, hr), pl.ds(hr, hr)
-
-    def turn(g, which, src, dst, device):
-        return remote(src, dst, y_send.at[g, which], y_recv.at[g, which], hist=device)
-
-    turns = [
+    def y_part(g, yy, i):
+        return kept[g, yy, i, :hp] + take[g, yy, i, :hp].astype(high)
+
+    def x_part(g, xx, i):
+        yy, j = lax.div(i, per), lax.rem(i, per)
+        some = pl.ds(pl.multiple_of(xx * lanes, lanes), lanes)
+        return kept[g, yy, j, hp:, some] + take[g, yy, j, hp:, some].astype(high)
+
+    def around(size, axis, me_on, bufs, send, recv, part, count, result):
+        far, to_next, to_prev, half_in, from_prev, from_next = bufs
+        nxt, prv = lax.rem(me_on + 1, size), lax.rem(me_on + size - 1, size)
+        across_it = lax.rem(me_on + 2, size)
+        q = hp // 2
+        top, bottom = pl.ds(0, q), pl.ds(q, q)
+        to = (
+            {"hist": right}, {"hist": left}
+        ) if axis == "y" else ({"rep": nxt}, {"rep": prv})
+
+        def turn(g, which, src, dst, device):
+            return remote(src, dst, send.at[g, which], recv.at[g, which], **device)
+
+        turns = [
+            [
+                turn(g, 0, far.at[g, :, top], half_in.at[g, :, top], to[0]),
+                turn(g, 1, far.at[g, :, bottom], half_in.at[g, :, bottom], to[1]),
+                turn(g, 2, to_next.at[g, :, bottom], from_prev.at[g, :, bottom], to[0]),
+                turn(g, 3, to_prev.at[g, :, top], from_next.at[g, :, top], to[1]),
+                turn(g, 4, to_next.at[g, :, top], from_prev.at[g, :, top], to[0]),
+                turn(g, 5, to_prev.at[g, :, bottom], from_next.at[g, :, bottom], to[1]),
+            ]
+            for g in range(GROUPS)
+        ]
+
+        def first(g):
+            def one(i, carry):
+                far[g, i] = part(g, across_it, i).astype(low)
+                to_next[g, i, bottom] = part(g, nxt, i)[q:].astype(low)
+                to_prev[g, i, top] = part(g, prv, i)[:q].astype(low)
+                return carry
+
+            lax.fori_loop(0, count, one, 0)
+            for m in range(4):
+                turns[g][m].start()
+
+        def second(g):
+            turns[g][0].wait_recv()
+            turns[g][1].wait_recv()
+
+            def one(i, carry):
+                up = part(g, nxt, i)[:q] + half_in[g, i, top].astype(high)
+                down = part(g, prv, i)[q:] + half_in[g, i, bottom].astype(high)
+                to_next[g, i, top] = up.astype(low)
+                to_prev[g, i, bottom] = down.astype(low)
+                return carry
+
+            lax.fori_loop(0, count, one, 0)
+            turns[g][4].start()
+            turns[g][5].start()
+
+        def last(g):
+            for m in (2, 3, 4, 5):
+                turns[g][m].wait_recv()
+
+            def one(i, carry):
+                result[g, i] = (
+                    part(g, me_on, i)
+                    + from_prev[g, i].astype(high)
+                    + from_next[g, i].astype(high)
+                )
+                return carry
+
+            lax.fori_loop(0, count, one, 0)
+
+        return turns, first, second, last
+
+    y_turns, y_first, y_second, y_last = around(
+        Y, "y", y, y_bufs, y_send, y_recv, y_part, per, y_sum
+    )
+    x_turns, x_first, x_second, x_last = around(
+        reps, "x", x, x_bufs, x_send, x_recv, x_part, Y * per, x_sum
+    )
+
+    def lanes_of(xx):
+        return pl.ds(pl.multiple_of(xx * lanes, lanes), lanes)
+
+    x_moves = [
         [
-            turn(g, 0, opposite.at[g, :, top], half_in.at[g, :, top], right),
-            turn(g, 1, opposite.at[g, :, low], half_in.at[g, :, low], left),
-            turn(g, 2, to_right.at[g, :, low], from_left.at[g, :, low], right),
-            turn(g, 3, to_left.at[g, :, top], from_right.at[g, :, top], left),
-            turn(g, 4, to_right.at[g, :, top], from_left.at[g, :, top], right),
-            turn(g, 5, to_left.at[g, :, low], from_right.at[g, :, low], left),
+            remote(
+                x_out.at[g, d], x_in.at[g, d], x_put.at[g, d], x_get.at[g, d], rep=others[d - 1]
+            )
+            for d in range(1, reps)
         ]
         for g in range(GROUPS)
     ]
-    y_right, y_left, y_far = lax.rem(y + 1, Y), lax.rem(y + Y - 1, Y), lax.rem(y + 2, Y)
-
-    def y_first(g):
+    y_moves = [
+        [
+            remote(
+                y_out.at[g, d], y_in.at[g, d], y_put.at[g, d], y_get.at[g, d], hist=ring[d - 1]
+            )
+            for d in range(1, Y)
+        ]
+        for g in range(GROUPS)
+    ]
+
+    def swap(g):
+        for d in range(1, reps):
+            x_out[g, d] = y_sum[g, :, :, lanes_of(others[d - 1])].astype(low)
+            x_moves[g][d - 1].start()
+        for d in range(1, Y):
+            y_out[g, d] = x_sum[g, pl.ds(lax.rem(y + d, Y) * per, per)].astype(low)
+            y_moves[g][d - 1].start()
+
+    def join(g):
+        total = y_sum[g, :, :, lanes_of(x)]
+        for d in range(1, reps):
+            x_moves[g][d - 1].wait_recv()
+            total = total + x_in[g, d].astype(high)
+        for i in range(per):
+            mine[0:planes // 2, g * per + i] = total[i].reshape(planes // 2, own_rows, lanes)
+        total = x_sum[g, pl.ds(y * per, per)]
+        for d in range(1, Y):
+            y_moves[g][d - 1].wait_recv()
+            total = total + y_in[g, d].astype(high)
+        for i in range(per):
+            mine[planes // 2:, g * per + i] = total[i].reshape(planes // 2, own_rows, lanes)
+
+    def first(g):
         pair[g].wait_recv()
-        kind = opposite.dtype
-
-        def one(i, carry):
-            opposite[g, i] = (kept[g, y_far, i] + take[g, y_far, i].astype(jnp.float32)).astype(kind)
-            right_sum = kept[g, y_right, i] + take[g, y_right, i].astype(jnp.float32)
-            left_sum = kept[g, y_left, i] + take[g, y_left, i].astype(jnp.float32)
-            to_right[g, i, low] = right_sum[hr:].astype(kind)
-            to_left[g, i, top] = left_sum[:hr].astype(kind)
-            kept[g, y_right, i] = right_sum
-            kept[g, y_left, i] = left_sum
-            return carry
-
-        lax.fori_loop(0, per, one, 0)
-        for m in range(4):
-            turns[g][m].start()
-
-    def y_second(g):
-        turns[g][0].wait_recv()
-        turns[g][1].wait_recv()
-
-        def one(i, carry):
-            up = kept[g, y_right, i, top] + half_in[g, i, top].astype(jnp.float32)
-            down = kept[g, y_left, i, low] + half_in[g, i, low].astype(jnp.float32)
-            to_right[g, i, top] = up.astype(to_right.dtype)
-            to_left[g, i, low] = down.astype(to_left.dtype)
-            return carry
-
-        lax.fori_loop(0, per, one, 0)
-        turns[g][4].start()
-        turns[g][5].start()
-
-    def y_last(g):
-        for m in (2, 3, 4, 5):
-            turns[g][m].wait_recv()
-
-        def one(i, carry):
-            total = kept[g, y, i] + take[g, y, i].astype(jnp.float32)
-            total = total + from_left[g, i].astype(jnp.float32)
-            total = total + from_right[g, i].astype(jnp.float32)
-            mine[:, g * per + i] = total.reshape(planes, own_rows, width)
-            return carry
-
-        lax.fori_loop(0, per, one, 0)
-
-    products(0)
-    grad_x_ref[...] = (
-        wide_g
-        + lax.dot_general(
-            dpre_ref[...], weights_ref[0], (((1,), (1,)), ((), ())),
-            preferred_element_type=jnp.float32,
-        )
-    ).astype(grad_x_ref.dtype)
-    for g in range(1, GROUPS):
-        products(g)
-        y_first(g - 1)
-        if g > 1:
-            y_second(g - 2)
-    y_first(GROUPS - 1)
-    if GROUPS > 1:
-        y_second(GROUPS - 2)
-    y_second(GROUPS - 1)
-    for g in range(GROUPS):
+        y_first(g)
+        x_first(g)
+
+    def second(g):
+        y_second(g)
+        x_second(g)
+
+    def last(g):
         y_last(g)
+        x_last(g)
+        swap(g)
+
+    def extra():
+        grad_x_ref[...] = (
+            wide_g
+            + lax.dot_general(
+                dpre_ref[...], weights_ref[0], (((1,), (1,)), ((), ())),
+                preferred_element_type=high,
+            )
+        ).astype(grad_x_ref.dtype)
+
+    stages = [products, first, second, last, join]
+    for step in range(GROUPS + len(stages) - 1):
+        for lag, stage in enumerate(stages):
+            if 0 <= step - lag < GROUPS:
+                stage(step - lag)
+        if step == 0:
+            extra()
 
     z_rows = mats * own_rows
 
     def stage_z(p, carry):
-        z_out[p, pl.ds(0, z_rows)] = mine[p].reshape(z_rows, width).astype(z_out.dtype)
+        z_out[p, pl.ds(0, z_rows)] = mine[p].reshape(z_rows, lanes).astype(low)
         return carry
 
     lax.fori_loop(0, planes, stage_z, 0)
@@ -588,27 +707,25 @@
         )
         copy.start()
         z_moves.append(copy)
-    total = mine[z].reshape(z_rows, width)
+    total = mine[z].reshape(z_rows, lanes)
     for d in range(1, planes):
         z_moves[d - 1].wait_recv()
-        total = total + z_in[d, pl.ds(0, z_rows)].astype(jnp.float32)
+        total = total + z_in[d, pl.ds(0, z_rows)].astype(high)
 
     share[x] = total
-    x_moves = []
+    share_moves = []
     for d in range(1, reps):
         copy = remote(
-            share.at[x], share.at[x], x_send.at[d], x_recv.at[d], rep=others[d - 1]
+            share.at[x], share.at[x], share_send.at[d], share_recv.at[d], rep=others[d - 1]
         )
         copy.start()
-        x_moves.append(copy)
-    for copy in x_moves:
+        share_moves.append(copy)
+    for copy in share_moves:
         copy.wait_recv()
-    total = share[0]
-    for d in range(1, reps):
-        total = total + share[d]
-    grad_w_ref[...] = total.reshape(grad_w_ref.shape)
-
-    for group in [pair, z_moves, x_moves] + turns:
+    for xx in range(reps):
+        grad_w_ref[:, :, xx * lanes:(xx + 1) * lanes] = share[xx].reshape(mats, own_rows, lanes)
+
+    for group in [pair, z_moves, share_moves] + y_turns + x_turns + x_moves + y_moves:
         for copy in group:
             copy.wait_send()
 
@@ -621,6 +738,8 @@
     own_rows = width // (planes * PLANE)
     per = mats // GROUPS
     piece = planes * own_rows
+    hp = piece // 2
+    lanes = width // reps
     z_pad = -(-mats * own_rows // 16) * 16
     low, high = features.dtype, jnp.float32
     dma = pltpu.SemaphoreType.DMA
@@ -635,7 +754,7 @@
         in_specs=[pl.BlockSpec(memory_space=pltpu.SMEM)] + [vmem] * 5,
         out_specs=(vmem, vmem, vmem),
         scratch_shapes=[
-            pltpu.VMEM((tile, per_tile * tile), low),
+            pltpu.VMEM((2 * tile, per_tile * tile), low),
             pltpu.VMEM((mats, batch, width), low),
             pltpu.VMEM((batch, width), high),
             pltpu.VMEM((batch, width), low),
@@ -643,20 +762,28 @@
             pltpu.VMEM((GROUPS, Y, per, piece, width), high),
             pltpu.VMEM((GROUPS, Y, per, piece, width), low),
             pltpu.VMEM((GROUPS, Y, per, piece, width), low),
-            pltpu.VMEM((GROUPS, per, piece, width), low),
-            pltpu.VMEM((GROUPS, per, piece, width), low),
-            pltpu.VMEM((GROUPS, per, piece, width), low),
-            pltpu.VMEM((GROUPS, per, piece, width), low),
-            pltpu.VMEM((GROUPS, per, piece, width), low),
-            pltpu.VMEM((GROUPS, per, piece, width), low),
-            pltpu.VMEM((planes, mats, own_rows, width), high),
-            pltpu.VMEM((planes, z_pad, width), low),
-            pltpu.VMEM((planes, z_pad, width), low),
-            pltpu.VMEM((reps, mats * own_rows, width), high),
+            [pltpu.VMEM((GROUPS, per, hp, width), low)] * 6,
+            [pltpu.VMEM((GROUPS, Y * per, hp, lanes), low)] * 6,
+            pltpu.VMEM((GROUPS, per, hp, width), high),
+            pltpu.VMEM((GROUPS, Y * per, hp, lanes), high),
+            pltpu.VMEM((GROUPS, reps, per, hp, lanes), low),
+            pltpu.VMEM((GROUPS, reps, per, hp, lanes), low),
+            pltpu.VMEM((GROUPS, Y, per, hp, lanes), low),
+            pltpu.VMEM((GROUPS, Y, per, hp, lanes), low),
+            pltpu.VMEM((planes, mats, own_rows, lanes), high),
+            pltpu.VMEM((planes, z_pad, lanes), low),
+            pltpu.VMEM((planes, z_pad, lanes), low),
+            pltpu.VMEM((reps, mats * own_rows, lanes), high),
             dma((GROUPS,)),
             dma((GROUPS,)),
             dma((GROUPS, 6)),
             dma((GROUPS, 6)),
+            dma((GROUPS, 6)),
+            dma((GROUPS, 6)),
+            dma((GROUPS, reps)),
+            dma((GROUPS, reps)),
+            dma((GROUPS, Y)),
+            dma((GROUPS, Y)),
             dma((planes,)),
             dma((planes,)),
             dma((reps,)),
@@ -671,7 +798,6 @@
 def on_device(
     planes, reps, features, history, blk_owner, blk_offset, blk_relation, adjacency, weights, cotangent
 ):
-    owners = blk_owner.reshape(-1)
     tiles = adjacency[0]
     tile_rows = tiles.shape[-1]
     width = weights.shape[-1]
@@ -680,8 +806,8 @@
 
     tiles_held = table.shape[0]
     table = table.reshape(tiles_held, CHUNKS, tile_rows // CHUNKS, width)
-    levels = rooms(planes, owners.shape[0])
-    words = requests(planes, levels, tiles_held, owners, blk_offset.reshape(-1))
+    levels = rooms(planes, blk_offset.shape[1])
+    words = requests(planes, levels, tiles_held, blk_owner[0], blk_offset)
     first, codes, top = ask(planes, reps, table, words)
     pulled = lax.switch(
         top[5, 0],

time: 272 us -> 208 us (0.76)
  Pallas kernels: 249 us -> 198 us
  between operations: 10.3 us -> 1.34 us
  other arithmetic: 3.33 us -> 0 us
    pallas_call x1, Pallas kernels: 144 us -> 125 us  [pull(): pl.pallas_call(functools.partial(gather_kernel, planes, far_room, near_ro...]
    pallas_call x1, Pallas kernels: 66.4 us -> 47.3 us  [layer(): pl.pallas_call(functools.partial(layer_kernel, planes, reps), out_shape=(...]
    pallas_call x1, Pallas kernels: 37.9 us -> 23.7 us  [ask(): pl.pallas_call(functools.partial(ask_kernel, planes, reps), out_shape=(ja...]
where the time goes in v3:
time: 208 us; the launch traced here: 207 us
  Pallas kernels  198 us (95%)
  local copies, waits for them, and re-layouts  7.81 us (4%)
    pallas_call x1, Pallas kernels, pull(): pl.pallas_call(functools.partial(gather_kernel, planes, far_room, near_ro...  125 us
    pallas_call x1, Pallas kernels, layer(): pl.pallas_call(functools.partial(layer_kernel, planes, reps), out_shape=(...  47.3 us
    pallas_call x1, Pallas kernels, ask(): pl.pallas_call(functools.partial(ask_kernel, planes, reps), out_shape=(ja...  23.7 us
    unnamed x6, local copies, waits for them, and re-layouts  5.13 us

profile of v3, /device:TPU:8, one launch (start us, length us, event | category | flops | bytes accessed | tf_op | source)
XLA Modules:
  0.0 207.2 jit_solution(13766423431418129716)
XLA Ops:
  0.6 0.0 copy-start
  0.6 1.5 copy.11.owner_ref
  2.1 2.2 %shard_map.103.code_ref = s32[8,128]{1,0:T(8,128)} custom-call(s32[16,1]{1,0:T(8,128)} %copy.11.owner_ref, s32[1,16]{1,0:T(1,128)} %offset_ref.1), custom_call_target="tpu_custom_call" | custom-call | tf_op jit(solution)/shard_map/pallas_call | solution.py:441
  4.3 23.7 %shard_map.104 = (bf16[128,16,512]{2,1,0:T(8,128)(2,1)}, s32[8,8,128]{2,1,0:T(8,128)S(1)}, s32[8,128]{1,0:T(8,128)}) custom-call(bf16[16,8,16,512]{3,2,1,0:T(8,128)(2,1)} %bitcast.11, s32[8,128]{1,0:T(8,128)} %shard_map.103.code_ref), custom_call_target="tpu_custom_call" | custom-call | tf_op jit(solution)/shard_map/pallas_call | solution.py:182
  28.0 1.2 slice.3
  29.9 0.0 copy-done
  29.9 124.9 %conditional.1 = (bf16[16,128,512]{2,1,0:T(8,128)(2,1)}) conditional(s32[]{:T(128)} %bitcast.2, (bf16[16,8,16,512]{3,2,1,0:T(8,128)(2,1)S(1)}, bf16[128,16,512]{2,1,0:T(8,128)(2,1)}, s32[8,8,128]{2,1,0:T(8,128)S(1)}) %tuple.28, (bf16[16,8,16,512]{3,2,1,0:T(8,128)(2,1)S(1)}, bf16[128,16,512]{2,1,0:T(8,128)(2,1)}, ...), branch_computations={%region_0.0_spmd, %region_1.0_spmd, %region_2.0_spmd, %region_3.0_... | conditional | bytes 8 | solution.py:812
  29.9 124.7 %branch_1_fun.1 = bf16[16,128,512]{2,1,0:T(8,128)(2,1)} custom-call(bf16[16,8,16,512]{3,2,1,0:T(8,128)(2,1)S(1)} %get-tuple-element.32.table_ref, bf16[128,16,512]{2,1,0:T(8,128)(2,1)} %get-tuple-element.33.first_ref, s32[8,8,128]{2,1,0:T(8,128)S(1)} %get-tuple-element.34.codes), custom_call_target="tpu_custom_call" | custom-call | tf_op jit(solution)/shard_map/cond/branch_1_fun/pallas_call | solution.py:336
  154.8 47.3 %shard_map.105 = (bf16[256,512]{1,0:T(8,128)(2,1)}, bf16[256,512]{1,0:T(8,128)(2,1)}, f32[9,8,512]{2,1,0:T(8,128)}) custom-call(s32[1,16]{1,0:T(1,128)} %relation_ref.1, bf16[16,128,512]{2,1,0:T(8,128)(2,1)} %get-tuple-element.62.pulled_ref, bf16[16,128,128]{2,1,0:T(8,128)(2,1)} %bitcast.17, bf16[256,512]{1,0:T(8,128)(2,1)} %bitcast.18, ...), custom_call_target="tpu_custom_call" | custom-call | tf_op jit(solution)/shard_map/pallas_call | solution.py:747
  202.1 0.9 pad
  203.0 0.9 copy.12
  203.9 1.7 copy.19
  205.6 1.7 copy.20
Async XLA Ops:
  0.6 29.2 %copy-start = (bf16[1,2048,512]{2,1,0:T(8,128)(2,1)S(1)}, bf16[1,2048,512]{2,1,0:T(8,128)(2,1)}, u32[]{:S(2)}) copy-start(bf16[1,2048,512]{2,1,0:T(8,128)(2,1)} %param.13) | copy-start | bytes 6291460

commit v4 on v3

--- a/solution.py
+++ b/solution.py
@@ -11,7 +11,10 @@
 CORES = 2
 PLANE = Y * CORES
 CHUNKS = 8
+LEVEL, FAR, NEAR, KIND, SPOT, TILE, SPARE = 0, 16, 32, 48, 64, 80, 96
 STRIDE = 3
+HELD = 2
+BEGIN, PASS, ACROSS = 7.3, 3.5, 1.5
 
 
 def position(index):
@@ -48,7 +51,7 @@
         pl.semaphore_signal(
             barrier, inc=1, device_id=device, device_id_type=pl.DeviceIdType.MESH
         )
-    pl.semaphore_wait(barrier, len(partners))
+    return lambda: pl.semaphore_wait(barrier, len(partners))
 
 
 def plane_moves(part, link, tiles, right, left, partner):
@@ -71,10 +74,12 @@
         moves[m].start()
 
 
-def pass_on(moves):
-    moves[0].wait_recv()
+def pass_on(moves, wait=True):
+    if wait:
+        moves[0].wait_recv()
     moves[3].start()
-    moves[1].wait_recv()
+    if wait:
+        moves[1].wait_recv()
     moves[4].start()
     moves[5].start()
     moves[6].start()
@@ -87,8 +92,8 @@
     moves[8].start()
 
 
-def plane_ready(moves):
-    for m in (2, 5, 6, 7, 8):
+def plane_ready(moves, own=True):
+    for m in (2, 5, 6, 7, 8) if own else (5, 6, 7, 8):
         moves[m].wait_recv()
 
 
@@ -108,16 +113,21 @@
     sign = 1 - 2 * c
     x = lax.axis_index("rep")
     tiles = table_ref.shape[0]
-    part = part_of(tab_ref, tiles)
-    load = pltpu.make_async_copy(table_ref.at[:, 0], part(0, 0), load_sem)
-    load.start()
     right, left, partner = hist(dy=1), hist(dy=-1), hist(dc=1)
     column = [hist(dz=sign * d) for d in range(1, planes)]
     plane = [hist(dy=d // CORES, dc=d % CORES) for d in range(1, PLANE)]
     others = [lax.rem(x + d, reps) for d in range(1, reps)]
-    greet(
+    all_here = greet(
         [{"hist": d} for d in column + plane] + [{"rep": d} for d in others]
     )
+    parts = [part_of(tab_ref.at[r], tiles) for r in range(HELD)]
+    loads = [
+        pltpu.make_async_copy(table_ref.at[:, r], parts[r](0, 0), load_sem.at[r])
+        for r in range(HELD)
+    ]
+    for copy in loads:
+        copy.start()
+    all_here()
 
     own = pltpu.make_async_copy(code_ref, codes.at[0], own_sem)
     own.start()
@@ -129,12 +139,17 @@
         copy.start()
         asks.append(copy)
 
-    def link(which, src, dst, device):
-        return remote(src, dst, ring_send.at[which], ring_recv.at[which], hist=device)
-
-    moves = plane_moves(part, link, tiles, right, left, partner)
-    load.wait()
-    own_out(moves)
+    moves = []
+    for r in range(HELD):
+        def link(which, src, dst, device, r=r):
+            return remote(
+                src, dst, ring_send.at[r, which], ring_recv.at[r, which], hist=device
+            )
+
+        moves.append(plane_moves(parts[r], link, tiles, right, left, partner))
+        loads[r].wait()
+        if r == 0:
+            own_out(moves[0])
 
     own.wait()
     for copy in asks:
@@ -150,7 +165,8 @@
         )
         copy.start()
         spread.append(copy)
-    pass_on(moves)
+    pass_on(moves[0])
+    own_out(moves[1])
     for d in range(1, PLANE):
         spread[d - 1].wait_recv()
         top = jnp.maximum(top, plane_flags[d])
@@ -162,14 +178,16 @@
         )
         copy.start()
         over.append(copy)
-    across(moves)
+    across(moves[0])
     for d in range(1, reps):
         over[d - 1].wait_recv()
         top = jnp.maximum(top, rep_flags[d])
-    level_ref[...] = top
-
-    plane_ready(moves)
-    for group in (asks, spread, over, moves):
+    level_ref[0, 0] = top[0, 0]
+
+    plane_ready(moves[0])
+    for m in (0, 1, 2):
+        moves[1][m].wait_recv()
+    for group in [asks, spread, over, moves[0], moves[1][:3]]:
         for copy in group:
             copy.wait_send()
 
@@ -182,28 +200,28 @@
     return pl.pallas_call(
         functools.partial(ask_kernel, planes, reps),
         out_shape=(
-            jax.ShapeDtypeStruct((PLANE * tiles, rows, width), table.dtype),
-            jax.ShapeDtypeStruct((planes, 8, 128), jnp.int32),
-            jax.ShapeDtypeStruct((8, 128), jnp.int32),
+            jax.ShapeDtypeStruct((HELD, PLANE * tiles, rows, width), table.dtype),
+            jax.ShapeDtypeStruct((planes, 1, 128), jnp.int32),
+            jax.ShapeDtypeStruct((1, 1), jnp.int32),
         ),
         in_specs=[pl.BlockSpec(memory_space=pl.ANY), vmem],
-        out_specs=(vmem, vmem, vmem),
+        out_specs=(vmem, vmem, pl.BlockSpec(memory_space=pltpu.SMEM)),
         scratch_shapes=[
-            words((2, 8, 128), jnp.int32),
-            words((PLANE, 8, 128), jnp.int32),
-            words((reps, 8, 128), jnp.int32),
+            words((2, 1, 128), jnp.int32),
+            words((PLANE, 1, 128), jnp.int32),
+            words((reps, 1, 128), jnp.int32),
             dma(()),
-            dma(()),
+            dma((HELD,)),
             dma((planes,)),
             dma((planes,)),
             dma((PLANE,)),
             dma((PLANE,)),
             dma((reps,)),
             dma((reps,)),
-            dma((9,)),
-            dma((9,)),
+            dma((HELD, 9)),
+            dma((HELD, 9)),
         ],
-        compiler_params=pltpu.CompilerParams(collective_id=0, has_side_effects=True),
+        compiler_params=pltpu.CompilerParams(collective_id=0, has_side_effects=True, vmem_limit_bytes=16 << 20),
     )(table, code)
 
 
@@ -219,18 +237,31 @@
     rows = table_ref.shape[2]
     slots = out_ref.shape[0]
 
-    loads = [pltpu.make_async_copy(first_ref, tabs[0], load_sem.at[0])] + [
-        pltpu.make_async_copy(
-            table_ref.at[:, r], tabs[r].at[pl.ds(0, tiles)], load_sem.at[r]
-        )
-        for r in range(1, CHUNKS)
-    ]
-    for copy in loads:
-        copy.start()
-
     right, left, partner = hist(dy=1), hist(dy=-1), hist(dc=1)
     ahead, behind = hist(dz=sign), hist(dz=-sign)
-    greet([{"hist": d} for d in (right, left, partner, ahead, behind)])
+    all_here = greet([{"hist": d} for d in (right, left, partner, ahead, behind)])
+    most, one = pl.ds(0, 3 * tiles), pl.ds(4 * tiles, tiles)
+    loads = [
+        [pltpu.make_async_copy(first_ref.at[0], tabs[0], load_sem.at[0])],
+        [
+            pltpu.make_async_copy(first_ref.at[1, most], tabs[1].at[most], load_sem.at[1]),
+            pltpu.make_async_copy(first_ref.at[1, one], tabs[1].at[one], load_sem.at[CHUNKS]),
+        ],
+    ] + [
+        [
+            pltpu.make_async_copy(
+                table_ref.at[:, r], tabs[r].at[pl.ds(0, tiles)], load_sem.at[r]
+            )
+        ]
+        for r in range(HELD, CHUNKS)
+    ]
+    for copies in loads:
+        for copy in copies:
+            copy.start()
+
+    def loaded(r):
+        for copy in loads[r]:
+            copy.wait()
 
     moves = [[]]
     for r in range(1, CHUNKS):
@@ -242,12 +273,16 @@
         moves.append(plane_moves(part_of(tabs[r], tiles), link, tiles, right, left, partner))
 
     def begin(r):
-        loads[r].wait()
+        loaded(r)
         own_out(moves[r])
+
+    def second():
+        loaded(1)
+        pass_on(moves[1], False)
 
     def fill(r, dst, slot, lane, count, merge):
         def body(i, carry):
-            code = codes[slot, lane, i]
+            code = codes[slot, 0, lane + i]
             tile = tabs[r][lax.rem(code, PLANE * tiles)]
             if merge:
                 tile = jnp.where(lax.div(code, PLANE * tiles) == z, tile, dst[i])
@@ -276,18 +311,18 @@
 
     def step(r, s):
         if s == 0:
-            fill(r, stage_far.at[r], planes - half, 0, far_room[0], False)
+            fill(r, stage_far.at[r], planes - half, FAR, far_room[0], False)
         else:
             far_moves[r][s - 1].wait_recv()
-            fill(r, far.at[r, s - 1], planes - half + s, 0, far_room[s], True)
+            fill(r, far.at[r, s - 1], planes - half + s, FAR, far_room[s], True)
         far_moves[r][s].start()
         if s < half - 1:
             distance = half - 1 - s
             if s == 0:
-                fill(r, stage_near.at[r], distance, 1, near_room[0], False)
+                fill(r, stage_near.at[r], distance, NEAR, near_room[0], False)
             else:
                 near_moves[r][s - 1].wait_recv()
-                fill(r, near.at[r, s - 1], distance, 1, near_room[s], True)
+                fill(r, near.at[r, s - 1], distance, NEAR, near_room[s], True)
             near_moves[r][s].start()
 
     def finish(r):
@@ -295,33 +330,30 @@
         far_moves[r][half - 1].wait_recv()
 
         def body(i, carry):
-            kind = codes[0, 2, i]
-            spot = codes[0, 3, i]
-            tile = tabs[r][codes[0, 4, i]]
+            kind = codes[0, 0, KIND + i]
+            spot = codes[0, 0, SPOT + i]
+            tile = tabs[r][codes[0, 0, TILE + i]]
             other = jnp.where(kind == 1, far_end[r][spot], near_end[r][spot])
             out_ref[i, pl.ds(r * rows, rows)] = jnp.where(kind == 0, tile, other)
             return carry
 
         lax.fori_loop(0, slots, body, 0, unroll=2)
 
-    def first():
-        loads[0].wait()
-
-    events = [(-9, first, ())]
+    events = [(-7, all_here, ()), (-5, second, ()), (-0.5, loaded, (0,))]
     for r in range(CHUNKS):
+        if r >= HELD:
+            events.append((half * r - BEGIN, begin, (r,)))
+            events.append((half * r - PASS, pass_on, (moves[r],)))
         if r:
-            events.append((half * (r - 1) + 0.5, pass_on, (moves[r],)))
-            events.append((half * (r - 1) + 2.5, across, (moves[r],)))
-            events.append((half * r - 0.5, plane_ready, (moves[r],)))
-        if r + 1 < CHUNKS:
-            events.append((half * (r - 1) + 0.6 if r else -8, begin, (r + 1,)))
+            events.append((half * r - ACROSS, across, (moves[r],)))
+            events.append((half * r - 0.5, plane_ready, (moves[r], r >= HELD)))
         for s in range(half):
             events.append((half * r + STRIDE * s + 0.01 * r, step, (r, s)))
         events.append((half * r + STRIDE * half + 0.7, finish, (r,)))
     for _, act, args in sorted(events, key=lambda e: e[0]):
         act(*args)
 
-    for group in moves + far_moves + near_moves:
+    for group in [moves[1][3:]] + moves[HELD:] + far_moves + near_moves:
         for copy in group:
             copy.wait_send()
 
@@ -346,7 +378,7 @@
             pltpu.VMEM((chunks, half - 2) + block, table.dtype),
             [pltpu.VMEM(block, table.dtype)] * chunks,
             [pltpu.VMEM(block, table.dtype)] * chunks,
-            dma((chunks,)),
+            dma((chunks + 1,)),
             dma((chunks, 9)),
             dma((chunks, 9)),
             dma((chunks, half)),
@@ -380,7 +412,7 @@
     slots = offset_ref.shape[1]
 
     def parse(k):
-        owner = owner_ref[k, 0]
+        owner = owner_ref[0, k]
         oz, oy, oc = position(owner)
         turn = lax.rem(oy - y + Y, Y)
         rel = jnp.where(turn == 0, 0, jnp.where(turn == 3, 1, jnp.where(turn == 1, 2, 3)))
@@ -395,8 +427,8 @@
     def tally(k, carry):
         away = parse(k)[2]
         count[away] += 1
-        words[0, k] = any_code
-        words[1, k] = any_code
+        words[0, FAR + k] = any_code
+        words[0, NEAR + k] = any_code
         return carry
 
     lax.fori_loop(0, slots, tally, 0)
@@ -420,17 +452,17 @@
             for end, cap in zip(ends, caps):
                 over = jnp.maximum(over, jnp.where(end > cap, 1, 0))
         level = level + over
-    words[5, 0] = level
+    words[0, LEVEL] = level
 
     def put(k, carry):
         code, tile, away = parse(k)
         spot = start[away]
         start[away] = spot + 1
         kind = jnp.where(away == 0, 0, jnp.where(away <= half, 1, 2))
-        words[jnp.where(kind == 0, 6, kind - 1), spot] = code
-        words[2, k] = kind
-        words[3, k] = jnp.where(kind == 0, 0, spot)
-        words[4, k] = tile
+        words[0, jnp.where(kind == 0, SPARE, jnp.where(kind == 1, FAR, NEAR)) + spot] = code
+        words[0, KIND + k] = kind
+        words[0, SPOT + k] = jnp.where(kind == 0, 0, spot)
+        words[0, TILE + k] = tile
         return carry
 
     lax.fori_loop(0, slots, put, 0)
@@ -440,7 +472,7 @@
     smem = pl.BlockSpec(memory_space=pltpu.SMEM)
     return pl.pallas_call(
         functools.partial(words_kernel, planes, levels, tiles),
-        out_shape=jax.ShapeDtypeStruct((8, 128), jnp.int32),
+        out_shape=jax.ShapeDtypeStruct((1, 128), jnp.int32),
         in_specs=[smem, smem],
         out_specs=smem,
         scratch_shapes=[pltpu.SMEM((planes,), jnp.int32), pltpu.SMEM((planes,), jnp.int32)],
@@ -448,6 +480,7 @@
 
 
 GROUPS = 3
+LAG = 1.1
 
 
 def layer_kernel(
@@ -456,7 +489,7 @@
     masked, stacked, pre_ref, dpre_ref, product, kept, give, take, y_bufs, x_bufs, y_sum, x_sum,
     x_out, x_in, y_out, y_in, mine, z_out, z_in, share,
     pair_send, pair_recv, y_send, y_recv, x_send, x_recv,
-    x_put, x_get, y_put, y_get, z_send, z_recv, share_send, share_recv,
+    x_put, x_get, y_put, y_get, z_send, z_recv, share_send, share_recv, weights_held, weights_sem,
 ):
     me, z, y, c, hist = place(planes)
     x = lax.axis_index("rep")
@@ -476,9 +509,11 @@
     column = [hist(dz=d) for d in range(1, planes)]
     ring = [hist(dy=d) for d in range(1, Y)]
     others = [lax.rem(x + d, reps) for d in range(1, reps)]
-    greet(
+    all_here = greet(
         [{"hist": d} for d in column + ring + [partner]] + [{"rep": d} for d in others]
     )
+    fetch = pltpu.make_async_copy(weights_ref, weights_held, weights_sem)
+    fetch.start()
 
     stacked[0] = features_ref[...]
     pack = 2
@@ -500,10 +535,11 @@
 
     lax.fori_loop(0, batch_tiles * relations // pack, mix, 0)
 
-    pre_ref[...] = jnp.dot(stacked[0], weights_ref[0], preferred_element_type=high)
+    fetch.wait()
+    pre_ref[...] = jnp.dot(stacked[0], weights_held[0], preferred_element_type=high)
 
     def project(j, carry):
-        pre_ref[...] += jnp.dot(stacked[j], weights_ref[j], preferred_element_type=high)
+        pre_ref[...] += jnp.dot(stacked[j], weights_held[j], preferred_element_type=high)
         return carry
 
     lax.fori_loop(1, mats, project, 0)
@@ -679,18 +715,21 @@
         grad_x_ref[...] = (
             wide_g
             + lax.dot_general(
-                dpre_ref[...], weights_ref[0], (((1,), (1,)), ((), ())),
+                dpre_ref[...], weights_held[0], (((1,), (1,)), ((), ())),
                 preferred_element_type=high,
             )
         ).astype(grad_x_ref.dtype)
 
+    all_here()
     stages = [products, first, second, last, join]
-    for step in range(GROUPS + len(stages) - 1):
-        for lag, stage in enumerate(stages):
-            if 0 <= step - lag < GROUPS:
-                stage(step - lag)
-        if step == 0:
-            extra()
+    extra_at = [(GROUPS - 0.5, -1, extra, ())]
+    timed = [
+        (g + LAG * lag, -lag, stage, (g,))
+        for lag, stage in enumerate(stages)
+        for g in range(GROUPS)
+    ]
+    for _, _, act, args in sorted(timed + extra_at, key=lambda e: e[:2]):
+        act(*args)
 
     z_rows = mats * own_rows
 
@@ -722,8 +761,10 @@
         share_moves.append(copy)
     for copy in share_moves:
         copy.wait_recv()
-    for xx in range(reps):
-        grad_w_ref[:, :, xx * lanes:(xx + 1) * lanes] = share[xx].reshape(mats, own_rows, lanes)
+    for i in range(own_rows):
+        for xx in range(reps):
+            at = i * width + xx * lanes
+            grad_w_ref[:, at:at + lanes] = share[xx, pl.ds(i, mats, stride=own_rows)]
 
     for group in [pair, z_moves, share_moves] + y_turns + x_turns + x_moves + y_moves:
         for copy in group:
@@ -749,9 +790,9 @@
         out_shape=(
             jax.ShapeDtypeStruct((batch, width), low),
             jax.ShapeDtypeStruct((batch, width), low),
-            jax.ShapeDtypeStruct((mats, own_rows, width), high),
+            jax.ShapeDtypeStruct((mats, own_rows * width), high),
         ),
-        in_specs=[pl.BlockSpec(memory_space=pltpu.SMEM)] + [vmem] * 5,
+        in_specs=[pl.BlockSpec(memory_space=pltpu.SMEM)] + [vmem] * 4 + [pl.BlockSpec(memory_space=pl.ANY)],
         out_specs=(vmem, vmem, vmem),
         scratch_shapes=[
             pltpu.VMEM((2 * tile, per_tile * tile), low),
@@ -788,11 +829,29 @@
             dma((planes,)),
             dma((reps,)),
             dma((reps,)),
+            pltpu.VMEM(weights.shape, low),
+            dma(()),
         ],
         compiler_params=pltpu.CompilerParams(
             collective_id=1, has_side_effects=True, vmem_limit_bytes=60 << 20
         ),
     )(relation, pulled, tiles, features, cotangent, weights)
+
+
+def hand_over_kernel(a_ref, b_ref, c_ref, a_out, b_out, c_out):
+    a_out[...] = a_ref[...]
+    b_out[...] = b_ref[...]
+    c_out[...] = c_ref[...]
+
+
+def hand_over(*results):
+    vmem = pl.BlockSpec(memory_space=pltpu.VMEM)
+    return pl.pallas_call(
+        hand_over_kernel,
+        out_shape=tuple(jax.ShapeDtypeStruct(r.shape, r.dtype) for r in results),
+        in_specs=[vmem] * 3,
+        out_specs=(vmem,) * 3,
+    )(*results)
 
 
 def on_device(
@@ -807,10 +866,10 @@
     tiles_held = table.shape[0]
     table = table.reshape(tiles_held, CHUNKS, tile_rows // CHUNKS, width)
     levels = rooms(planes, blk_offset.shape[1])
-    words = requests(planes, levels, tiles_held, blk_owner[0], blk_offset)
+    words = requests(planes, levels, tiles_held, blk_owner.reshape(1, -1), blk_offset)
     first, codes, top = ask(planes, reps, table, words)
     pulled = lax.switch(
-        top[5, 0],
+        top[0, 0],
         [
             functools.partial(pull, planes, level, far_room, near_room)
             for level, (far_room, near_room) in enumerate(levels)
@@ -820,7 +879,8 @@
     fresh, grad_x, grad_w = layer(
         planes, reps, blk_relation, pulled, tiles, features[0], cotangent[0], weights
     )
-    return fresh[None], grad_x[None], grad_w.reshape(mats, -1)
+    fresh, grad_x, grad_w = hand_over(fresh, grad_x, grad_w)
+    return fresh[None], grad_x[None], grad_w
 
 
 def solution(mesh):

time: 208 us -> 193 us (0.928)
  local copies, waits for them, and re-layouts: 7.81 us -> 0.65 us
  Pallas kernels: 198 us -> 191 us
    pallas_call x1, Pallas kernels: 125 us -> 116 us  [pull(): pl.pallas_call(functools.partial(gather_kernel, planes, far_room, near_ro...]
    unnamed x6 -> x4, local copies, waits for them, and re-layouts: 5.13 us -> 0.65 us
    pallas_call x1, Pallas kernels: 47.3 us -> 43.1 us  [layer(): pl.pallas_call(functools.partial(layer_kernel, planes, reps), out_shape=(...]
    pallas_call x1, Pallas kernels: 23.7 us -> 27.6 us  [ask(): pl.pallas_call(functools.partial(ask_kernel, planes, reps), out_shape=(ja...]
where the time goes in v4:
time: 193 us
  Pallas kernels  191 us (99%)
    pallas_call x1, Pallas kernels, pull(): pl.pallas_call(functools.partial(gather_kernel, planes, far_room, near_ro...  116 us
    pallas_call x1, Pallas kernels, layer(): pl.pallas_call(functools.partial(layer_kernel, planes, reps), out_shape=(...  43.1 us
    pallas_call x1, Pallas kernels, ask(): pl.pallas_call(functools.partial(ask_kernel, planes, reps), out_shape=(ja...  27.6 us

profile of v4, /device:TPU:8, one launch (start us, length us, event | category | flops | bytes accessed | tf_op | source)
XLA Modules:
  0.0 192.9 jit_solution(12825821338314693491)
XLA Ops:
  0.6 1.9 %shard_map.103.code_ref = s32[1,128]{1,0:T(1,128)} custom-call(s32[1,16]{1,0:T(1,128)} %bitcast.18, s32[1,16]{1,0:T(1,128)} %offset_ref.1), custom_call_target="tpu_custom_call" | custom-call | tf_op jit(solution)/shard_map/pallas_call | solution.py:473
  2.6 0.0 copy-start
  2.6 0.6 copy-done
  3.2 0.0 copy-start.1
  3.2 27.6 %shard_map.104 = (bf16[2,128,16,512]{3,2,1,0:T(8,128)(2,1)}, s32[8,1,128]{2,1,0:T(1,128)S(1)}, s32[1,1]{1,0:T(1,128)}) custom-call(bf16[16,8,16,512]{3,2,1,0:T(8,128)(2,1)} %bitcast.8, s32[1,128]{1,0:T(1,128)S(1)} %copy-done), custom_call_target="tpu_custom_call" | custom-call | tf_op jit(solution)/shard_map/pallas_call | solution.py:200
  31.4 0.0 copy-done.1
  31.5 116.3 %conditional.1 = (bf16[16,128,512]{2,1,0:T(8,128)(2,1)}) conditional(s32[]{:T(128)} %bitcast.2, (bf16[16,8,16,512]{3,2,1,0:T(8,128)(2,1)S(1)}, bf16[2,128,16,512]{3,2,1,0:T(8,128)(2,1)}, s32[8,1,128]{2,1,0:T(1,128)S(1)}) %tuple.26, (bf16[16,8,16,512]{3,2,1,0:T(8,128)(2,1)S(1)}, bf16[2,128,16,512]{3,2,1,0:T(8,128)(2,1)}, ...), branch_computations={%region_0.0_spmd, %region_1.0_spmd, %region_2.0_spmd, %region_3.0_... | conditional | bytes 8 | solution.py:871
  31.5 116.1 %branch_1_fun.1 = bf16[16,128,512]{2,1,0:T(8,128)(2,1)} custom-call(bf16[16,8,16,512]{3,2,1,0:T(8,128)(2,1)S(1)} %get-tuple-element.32.table_ref, bf16[2,128,16,512]{3,2,1,0:T(8,128)(2,1)} %get-tuple-element.33.first_ref, s32[8,1,128]{2,1,0:T(1,128)S(1)} %get-tuple-element.34.codes), custom_call_target="tpu_custom_call" | custom-call | tf_op jit(solution)/shard_map/cond/branch_1_fun/pallas_call | solution.py:368
  147.8 43.1 %shard_map.105 = (bf16[256,512]{1,0:T(8,128)(2,1)}, bf16[256,512]{1,0:T(8,128)(2,1)}, f32[9,4096]{1,0:T(8,128)}) custom-call(s32[1,16]{1,0:T(1,128)} %relation_ref.1, bf16[16,128,512]{2,1,0:T(8,128)(2,1)} %get-tuple-element.62.pulled_ref, bf16[16,128,128]{2,1,0:T(8,128)(2,1)} %bitcast.13, bf16[256,512]{1,0:T(8,128)(2,1)} %bitcast.14, ...), custom_call_target="tpu_custom_call" | custom-call | tf_op jit(solution)/shard_map/pallas_call | solution.py:788
  190.9 2.0 %shard_map.106 = (bf16[256,512]{1,0:T(8,128)(2,1)}, bf16[256,512]{1,0:T(8,128)(2,1)}, f32[9,4096]{1,0:T(8,128)}) custom-call(bf16[256,512]{1,0:T(8,128)(2,1)} %get-tuple-element.56.a_ref, bf16[256,512]{1,0:T(8,128)(2,1)} %get-tuple-element.57.b_ref, f32[9,4096]{1,0:T(8,128)} %get-tuple-element.58.c_ref), custom_call_target="tpu_custom_call" | custom-call | tf_op jit(solution)/shard_map/pallas_call | solution.py:849
Async XLA Ops:
  2.6 0.7 copy-start
  3.2 28.2 %copy-start.1 = (bf16[1,2048,512]{2,1,0:T(8,128)(2,1)S(1)}, bf16[1,2048,512]{2,1,0:T(8,128)(2,1)}, u32[]{:S(2)}) copy-start(bf16[1,2048,512]{2,1,0:T(8,128)(2,1)} %param.13) | copy-start | bytes 6291460
